TPU v7x, 256 devices: a whole 4x4x8 slice. The times are simulated.
256 devices in a mesh: tensor: 4 (over x), expert: 64 (over z, y, core).
Axes of the slice: x: 4, y: 4, z: 8, core: 2. Of those that a mesh axis runs over, the one named last changes fastest.
Arguments:
- attn_out: bfloat16 [8192, 2048], P('expert', 'tensor'), may hold values from -6 to 6
- out_proj: bfloat16 [2048, 2048], P('tensor'), may hold values from -0.125 to 0.125
- hidden_in: bfloat16 [8192, 2048], P('expert')
- norm_gain: bfloat16 [2048], replicated, may hold values from 0.099609375 to 1.8984375
- router: bfloat16 [2048, 64], replicated, may hold values from -0.0625 to 0.0625
- routes: int32 [8192, 8], P('expert'), may hold values from 0 to 63, all different within a row; in each aligned block of 128 rows (0 to 127, 128 to 255, ...) at most 32 rows name the same one
- w_gate: bfloat16 [64, 2048, 1024], P('expert', None, 'tensor'), may hold values from -0.25 to 0.25
- w_up: bfloat16 [64, 2048, 1024], P('expert', None, 'tensor'), may hold values from -0.25 to 0.25
- w_down: bfloat16 [64, 1024, 2048], P('expert', 'tensor'), may hold values from -0.375 to 0.375
- final_gain: bfloat16 [2048], P('tensor'), may hold values from 0.099609375 to 1.8984375
- source: int32 [8192], P('expert'), may hold values from 0 to 8191, as said below
Outputs:
- mixed: bfloat16 [8192, 2048], P('expert', 'tensor')
Inputs may be any that keep to these rules, and one draw needn't show every extreme that they name: `routes`: each row names 8 different experts. In each aligned block of 128 rows no expert is named by more than 32 rows, a bound that some block reaches. source is a permutation. Each aligned block of 128 requests takes exactly 2 rows from each aligned block of 128 rows.
All inputs are finite; a program needn't handle non-finite values.
Results may differ from a plain program's by a relative error of at most 0.007.
Values may be sent and summed in bfloat16 or wider, within the bound.
A program may use at most 128 MiB of HBM per device.

v0:
```python
import jax
import jax.numpy as jnp
from jax import lax
from jax.sharding import PartitionSpec as P

epsilon = 1e-06


def rms_normalize(values, gain):
    floats = values.astype(jnp.float32)
    inverse_rms = lax.rsqrt(jnp.mean(floats * floats, axis=-1, keepdims=True) + epsilon)
    return floats * inverse_rms * gain.astype(jnp.float32)


def swiglu_rows(row_block, gate_matrix, up_matrix, down_matrix):
    gate_part = jnp.dot(row_block, gate_matrix, preferred_element_type=jnp.float32)
    up_part = jnp.dot(row_block, up_matrix, preferred_element_type=jnp.float32)
    activated = (jax.nn.silu(gate_part) * up_part).astype(jnp.bfloat16)
    return jnp.dot(activated, down_matrix, preferred_element_type=jnp.float32)


def on_device(
    attn_out,
    out_proj,
    hidden_in,
    norm_gain,
    router,
    routes,
    w_gate,
    w_up,
    w_down,
    final_gain,
    source,
):
    rows_dev = hidden_in.shape[0]
    model_width = hidden_in.shape[1]
    tensor_count = lax.axis_size("tensor")
    peer_count = lax.axis_size("expert")
    exp_dev = w_gate.shape[0]
    experts = exp_dev * peer_count
    top_count = routes.shape[1]
    capacity = min(rows_dev, 2 * rows_dev * top_count // experts)
    peer_rows = rows_dev // peer_count
    feature_share = model_width // tensor_count
    feature_first = lax.axis_index("tensor") * feature_share
    needed_block = source // rows_dev
    needed_local = source % rows_dev
    arrange = jnp.argsort(
        needed_block * rows_dev + jnp.arange(rows_dev, dtype=jnp.int32), stable=True
    )
    wanted = needed_local[arrange].reshape(peer_count, peer_rows)
    asked = lax.all_to_all(wanted, "expert", split_axis=0, concat_axis=0, tiled=True)
    head_term = jnp.dot(attn_out, out_proj, preferred_element_type=jnp.float32)
    attention = lax.psum(head_term, "tensor")
    residual = (hidden_in.astype(jnp.float32) + attention).astype(jnp.bfloat16)
    normed = rms_normalize(residual, norm_gain).astype(jnp.bfloat16)
    logits = jnp.dot(normed, router, preferred_element_type=jnp.float32)
    chosen = jnp.take_along_axis(logits, routes, axis=1)
    powers = jnp.exp(chosen)
    gate_weights = powers / jnp.sum(powers, axis=1, keepdims=True)
    pair_count = rows_dev * top_count
    flat_expert = routes.reshape(pair_count)
    onehot = (flat_expert[:, None] == jnp.arange(experts, dtype=jnp.int32)[None, :]).astype(
        jnp.int32
    )
    within_rank = jnp.sum((jnp.cumsum(onehot, axis=0) - 1) * onehot, axis=1)
    slot_index = flat_expert * capacity + within_rank
    pair_row = jnp.arange(pair_count, dtype=jnp.int32) // top_count
    slot_row = jnp.full((experts * capacity,), rows_dev, jnp.int32).at[slot_index].set(pair_row)
    extended = jnp.concatenate([normed, jnp.zeros((1, model_width), jnp.bfloat16)], axis=0)
    outgoing = extended[slot_row].reshape(peer_count, exp_dev, capacity, model_width)
    incoming = lax.all_to_all(outgoing, "expert", split_axis=0, concat_axis=0, tiled=True)
    slot_count = incoming.shape[2]
    row_block = incoming[:, 0].reshape(peer_count * slot_count, model_width)
    expert_rows = swiglu_rows(row_block, w_gate[0], w_up[0], w_down[0])
    results = [expert_rows.reshape(peer_count, slot_count, model_width)]
    partial_value = jnp.stack(results, axis=1)
    returned = lax.all_to_all(partial_value, "expert", split_axis=0, concat_axis=0, tiled=True)
    flat_back = returned.reshape(experts * capacity, returned.shape[3])
    picked = flat_back[slot_index].reshape(rows_dev, top_count, returned.shape[3])
    mixture = jnp.sum(gate_weights[:, :, None] * picked, axis=1)
    mixture = lax.psum_scatter(mixture, "tensor", scatter_dimension=1, tiled=True)
    residual_mine = lax.dynamic_slice_in_dim(residual, feature_first, feature_share, 1)
    total_mine = residual_mine.astype(jnp.float32) + mixture
    squares = lax.psum(jnp.sum(total_mine * total_mine, axis=-1), "tensor")
    inverse_rms = lax.rsqrt(squares / model_width + epsilon)[:, None]
    normalized = (total_mine * inverse_rms * final_gain.astype(jnp.float32)).astype(jnp.bfloat16)
    packed = normalized[asked.reshape(rows_dev)].reshape(peer_count, peer_rows, feature_share)
    arrived = lax.all_to_all(packed, "expert", split_axis=0, concat_axis=0, tiled=True)
    flat_arrived = arrived.reshape(rows_dev, feature_share)
    return jnp.zeros((rows_dev, feature_share), jnp.bfloat16).at[arrange].set(flat_arrived)


def solution(mesh):
    placed = (
        P("expert", "tensor"),
        P("tensor", None),
        P("expert", None),
        P(),
        P(),
        P("expert", None),
        P("expert", None, "tensor"),
        P("expert", None, "tensor"),
        P("expert", "tensor", None),
        P("tensor"),
        P("expert"),
    )
    return jax.shard_map(
        on_device, mesh=mesh, in_specs=placed, out_specs=P("expert", "tensor"), check_vma=False
    )
```

profile of v0, /device:TPU:1, one launch (start us, length us, event | category | flops | bytes accessed | tf_op | source)
XLA Modules:
  0.0 754.2 jit_solution(2453750161692147448)
XLA Ops:
  6.5 1.6 copy-done
  8.1 2.4 fusion.22
  10.5 0.7 broadcast_multiply_fusion
  11.2 0.8 copy.40
  12.0 0.1 eq.31
  12.1 0.1 eq.27
  12.2 0.7 convert_element_type.36
  12.9 0.1 copy.39
  13.0 0.1 mul.88
  13.1 18.0 %reduce-window.6 = s32[64,8,128]{2,1,0:T(8,128)S(1)} reduce-window(s32[64,8,128]{2,1,0:T(8,128)S(1)} %fusion.11, s32[]{:T(128)} %constant.81.clone.1), window={size=1x1x128 pad=0_0x0_0x127_0}, to_apply=%region_4.5 | reduce-window | flops 8323072 | bytes 524292 | tf_op jit(solution)/shard_map/reduce-window
  31.1 0.1 slice.18
  31.3 0.1 copy.42
  31.4 0.1 copy.43
  31.5 0.1 add_add_fusion
  31.7 0.1 fusion.10
  31.8 4.3 scatter_custom_fusion
  36.1 28.0 %all-reduce.3.cloned.1.call-done = f32[128,2048]{1,0:T(8,128)} async-done(((f32[128,2048]{1,0:T(8,128)}), f32[128,2048]{1,0:T(8,128)}) %all-reduce.3.cloned.1.call-update) | async-done | bytes 1048592 | tf_op jit(solution)/shard_map/psum | solution.py:54
  64.1 1.6 fusion.2
  65.7 0.2 fusion.4
  65.9 11.0 %gather_fusion = bf16[2048,2048]{1,0:T(8,128)(2,1)} fusion(bf16[129,2048]{1,0:T(8,128)(2,1)S(1)} %concatenate.3, s32[2048]{0:T(1024)S(1)} %fusion.14), kind=kCustom, calls=%fused_computation | custom fusion | bytes 16785408 | tf_op jit(solution)/shard_map/gather | solution.py:71
  77.0 196.7 %all_to_all.24 = bf16[64,1,32,2048]{3,2,1,0:T(8,128)(2,1)S(1)} all-to-all(bf16[64,1,32,2048]{3,2,1,0:T(8,128)(2,1)} %bitcast.56), channel_id=1, replica_groups=mesh['tensor'=4,'expert'=64] {'expert'}, dimensions={0} | all-to-all | bytes 16777216 | tf_op jit(solution)/shard_map/all_to_all | solution.py:72
  273.7 2.4 fusion.7
  276.0 2.6 fusion.1
  278.7 8.1 %convolution_bitcast_fusion = f32[64,1,32,2048]{3,2,1,0:T(8,128)} fusion(bf16[64,32,256]{2,1,0:T(8,128)(2,1)S(1)} %bitcast.59, bf16[1,256,2048]{2,1,0:T(8,128)(2,1)S(1)} %copy-done.2), kind=kOutput, calls=%fused_computation.9 | convolution fusion | flops 2147483648 | bytes 18874368 | tf_op jit(solution)/shard_map/dot_general | solution.py:19
  286.7 7.7 %all-to-all-start.1 = ((f32[64,1,32,2048]{3,2,1,0:T(8,128)}), f32[64,1,32,2048]{3,2,1,0:T(8,128)}, u32[]{:S(2)}, u32[]{:S(2)}) async-start(f32[64,1,32,2048]{3,2,1,0:T(8,128)} %convolution_bitcast_fusion), calls=%async_computation.1 | async-start | bytes 33554432 | tf_op jit(solution)/shard_map/all_to_all | solution.py:78
  294.5 0.1 copy.36
  294.6 0.1 reshape.178
  294.7 0.3 fusion.23
  295.0 7.0 gather_fusion.4
  302.1 0.1 reshape.181
  302.2 0.1 copy.38
  302.4 356.7 %all-to-all-done.1 = f32[64,1,32,2048]{3,2,1,0:T(8,128)} async-done(((f32[64,1,32,2048]{3,2,1,0:T(8,128)}), f32[64,1,32,2048]{3,2,1,0:T(8,128)}, u32[]{:S(2)}, u32[]{:S(2)}) %all-to-all-start.1) | async-done | bytes 16777248 | tf_op jit(solution)/shard_map/all_to_all | solution.py:78
  659.1 14.9 %gather_fusion.1 = f32[1024,2048]{1,0:T(8,128)} fusion(f32[2048,2048]{1,0:T(8,128)} %bitcast.15, s32[1024]{0:T(1024)S(1)} %broadcast_clamp_fusion), kind=kCustom, calls=%fused_computation.1 | custom fusion | bytes 16781312 | tf_op jit(solution)/shard_map/gather | solution.py:80
  674.0 7.4 fusion
  681.5 2.5 sort.17
  684.0 1.2 gather_fusion.2
  685.2 0.8 all_to_all.17
  686.0 14.6 %all-to-all-start.2 = ((s32[64,1,2]{2,1,0:T(1,128)}), s32[64,1,2]{2,1,0:T(1,128)S(1)}, u32[]{:S(2)}, u32[]{:S(2)}) async-start(s32[64,1,2]{2,1,0:T(1,128)} %bitcast.17), calls=%async_computation.3 | async-start | bytes 65536 | tf_op jit(solution)/shard_map/all_to_all | solution.py:52
  700.6 9.3 %all-to-all-done.2 = s32[64,1,2]{2,1,0:T(1,128)S(1)} async-done(((s32[64,1,2]{2,1,0:T(1,128)}), s32[64,1,2]{2,1,0:T(1,128)S(1)}, u32[]{:S(2)}, u32[]{:S(2)}) %all-to-all-start.2) | async-done | bytes 544 | tf_op jit(solution)/shard_map/all_to_all | solution.py:52
  709.9 0.5 broadcast.191
  710.4 0.7 reduce.3
  711.2 0.1 reshape.143
  711.4 1.1 multiply_reduce_fusion
  712.4 7.6 %psum.15 = f32[128]{0:T(128)S(1)} all-reduce(f32[128]{0:T(128)S(1)} %multiply_reduce_fusion), channel_id=1, replica_groups=mesh['tensor'=4,'expert'=64] {'tensor'}, use_global_device_ids=true, to_apply=%region_11.12 | all-reduce | flops 128 | bytes 1024 | tf_op jit(solution)/shard_map/psum | solution.py:85
  720.1 1.0 multiply_convert_fusion
  721.1 0.8 gather_fusion.3
  722.0 23.6 %all_to_all.25 = bf16[64,2,512]{2,1,0:T(2,128)(2,1)S(1)} all-to-all(bf16[64,2,512]{2,1,0:T(2,128)(2,1)S(1)} %reshape.144), channel_id=1, replica_groups=mesh['tensor'=4,'expert'=64] {'expert'}, dimensions={0} | all-to-all | bytes 262144 | tf_op jit(solution)/shard_map/all_to_all | solution.py:89
  745.7 1.7 scatter_custom_fusion.1
  (45 shorter events, 0.5 us)
Async XLA Ops:
  6.5 1.6 copy-start
  6.5 57.5 %all-reduce.3.cloned.1.call-start = ((), (), s32[]{:S(2)}) async-start(), calls=%async_computation.5 | async-start | bytes 2097152 | tf_op jit(solution)/shard_map/psum | solution.py:54
  76.9 196.7 %copy-start.6 = (bf16[1,2048,256]{2,1,0:T(8,128)(2,1)S(1)}, bf16[1,2048,256]{2,1,0:T(8,128)(2,1)}, u32[]{:S(2)}) copy-start(bf16[1,2048,256]{2,1,0:T(8,128)(2,1)} %param.17) | copy-start | bytes 3145732
  273.6 2.4 copy-start.7
  276.0 2.7 copy-start.2
  286.7 7.7 %copy-start.4 = (s32[128,8]{0,1:T(8,128)S(1)}, s32[128,8]{0,1:T(8,128)}, u32[]{:S(2)}) copy-start(s32[128,8]{0,1:T(8,128)} %param.16) | copy-start | bytes 12292
  286.7 8.0 %copy-start.3 = (bf16[2048,64]{0,1:T(8,128)(2,1)S(1)}, bf16[2048,64]{0,1:T(8,128)(2,1)}, u32[]{:S(2)}) copy-start(bf16[2048,64]{0,1:T(8,128)(2,1)} %param.15) | copy-start | bytes 786436
  286.7 372.3 %all-to-all-start.1 = ((f32[64,1,32,2048]{3,2,1,0:T(8,128)}), f32[64,1,32,2048]{3,2,1,0:T(8,128)}, u32[]{:S(2)}, u32[]{:S(2)}) async-start(f32[64,1,32,2048]{3,2,1,0:T(8,128)} %convolution_bitcast_fusion), calls=%async_computation.1 | async-start | bytes 33554432 | tf_op jit(solution)/shard_map/all_to_all | solution.py:78
  294.4 416.9 %reduce-scatter.2.cloned.1.call-start = ((), (), s32[]{:S(2)}) async-start(), calls=%async_computation.6 | async-start | bytes 1310720 | tf_op jit(solution)/shard_map/reduce_scatter | solution.py:82
  659.1 88.3 %copy-start.1 = (bf16[512,2048]{1,0:T(8,128)(2,1)S(1)}, bf16[512,2048]{1,0:T(8,128)(2,1)}, u32[]{:S(2)}) copy-start(bf16[512,2048]{1,0:T(8,128)(2,1)} %param.12) | copy-start | bytes 6291460
  674.0 7.4 copy-start.8
  674.0 26.6 %copy-start.5 = (bf16[512]{0:T(512)(128)(2,1)S(1)}, bf16[512]{0:T(512)(128)(2,1)}, u32[]{:S(2)}) copy-start(bf16[512]{0:T(512)(128)(2,1)} %param.20) | copy-start | bytes 3076
  686.0 23.9 %all-to-all-start.2 = ((s32[64,1,2]{2,1,0:T(1,128)}), s32[64,1,2]{2,1,0:T(1,128)S(1)}, u32[]{:S(2)}, u32[]{:S(2)}) async-start(s32[64,1,2]{2,1,0:T(1,128)} %bitcast.17), calls=%async_computation.3 | async-start | bytes 65536 | tf_op jit(solution)/shard_map/all_to_all | solution.py:52
Sparse Core Ops, SparseCore 0:
  10.7 53.3 all-reduce.2
  681.5 29.5 reduce-scatter.1
where the time goes:
time: 755 us; the launch traced here: 754 us
  waiting for transfers between devices  394 us (52%)
  blocking collectives  228 us (30%)
  local copies, waits for them, and re-layouts  46.1 us (6%)
  other arithmetic  34.4 us (5%)
  starting transfers between devices  22.3 us (3%)
  matrix products  15.7 us (2%)
  between operations  13.7 us (2%)
    all_to_all x1, waiting for transfers between devices, on_device(): lax.all_to_all(partial_value, 'expert', split_axis=0, concat_axis=0, tile...  357 us
    all_to_all x1, blocking collectives, on_device(): lax.all_to_all(outgoing, 'expert', split_axis=0, concat_axis=0, tiled=True)  197 us
    psum x1, waiting for transfers between devices, on_device(): attention = lax.psum(head_term, 'tensor')  28 us
    all_to_all x1, blocking collectives, on_device(): lax.all_to_all(packed, 'expert', split_axis=0, concat_axis=0, tiled=True)  23.6 us
    another operation x2, other arithmetic  18 us
  transfers between devices with their start and end apart: 4, of which 3 were waited for; matrix products, arithmetic and copies ran while one was open for 5% of the time, Pallas kernels for 0%

commit v1 on v0

v1 whole, which is shorter than its diff:
```python
import jax
import jax.numpy as jnp
from jax import lax
from jax.sharding import PartitionSpec as P

epsilon = 1e-06


def rms_normalize(values, gain):
    floats = values.astype(jnp.float32)
    inverse_rms = lax.rsqrt(jnp.mean(floats * floats, axis=-1, keepdims=True) + epsilon)
    return floats * inverse_rms * gain.astype(jnp.float32)


def on_device(
    attn_out,
    out_proj,
    hidden_in,
    norm_gain,
    router,
    routes,
    w_gate,
    w_up,
    w_down,
    final_gain,
    source,
):
    rows_dev, model_width = hidden_in.shape
    tensor_count = lax.axis_size("tensor")
    peer_count = lax.axis_size("expert")
    experts = peer_count
    top_count = routes.shape[1]
    capacity = min(rows_dev, 2 * rows_dev * top_count // experts)
    slots = capacity // tensor_count
    peer_rows = rows_dev // peer_count
    feature_share = model_width // tensor_count
    plane = lax.axis_index("tensor")
    feature_first = plane * feature_share
    needed_block = source // rows_dev
    needed_local = source % rows_dev

    same = needed_block[:, None] == needed_block[None, :]
    earlier = jnp.arange(rows_dev)[None, :] < jnp.arange(rows_dev)[:, None]
    turn = jnp.sum((same & earlier).astype(jnp.int32), axis=1)
    place = needed_block * peer_rows + turn
    places = place[:, None] == jnp.arange(rows_dev)[None, :]
    wanted = jnp.sum(jnp.where(places, needed_local[:, None], 0), axis=0).reshape(
        peer_count, peer_rows
    )
    asked = lax.all_to_all(wanted, "expert", split_axis=0, concat_axis=0, tiled=True)

    gate_all = lax.all_gather(w_gate[0], "tensor")
    up_all = lax.all_gather(w_up[0], "tensor")
    down_all = lax.all_gather(w_down[0], "tensor")

    head_term = jnp.dot(attn_out, out_proj, preferred_element_type=jnp.float32)
    attention = lax.psum(head_term, "tensor")
    residual = (hidden_in.astype(jnp.float32) + attention).astype(jnp.bfloat16)
    normed = rms_normalize(residual, norm_gain).astype(jnp.bfloat16)
    logits = jnp.dot(normed, router, preferred_element_type=jnp.float32)

    named = jnp.any(routes[:, :, None] == jnp.arange(experts)[None, None, :], axis=1)
    powers = jnp.where(named, jnp.exp(logits), 0.0)
    gate_weights = powers / jnp.sum(powers, axis=1, keepdims=True)
    before = (jnp.arange(rows_dev)[None, :] < jnp.arange(rows_dev)[:, None]).astype(jnp.bfloat16)
    rank = jnp.dot(before, named.astype(jnp.bfloat16), preferred_element_type=jnp.float32)
    rank = rank.astype(jnp.int32) - plane * slots
    taken = named[:, :, None] & (rank[:, :, None] == jnp.arange(slots)[None, None, :])
    taken = taken.reshape(rows_dev, experts * slots)
    outgoing = lax.dot_general(
        taken.astype(jnp.bfloat16),
        normed,
        (((0,), (0,)), ((), ())),
        preferred_element_type=jnp.float32,
    ).astype(jnp.bfloat16)
    outgoing = outgoing.reshape(peer_count, slots, model_width)
    incoming = lax.all_to_all(outgoing, "expert", split_axis=0, concat_axis=0, tiled=True)
    row_block = incoming.reshape(peer_count * slots, model_width)

    gate_part = jnp.einsum("sd,qdf->sqf", row_block, gate_all, preferred_element_type=jnp.float32)
    up_part = jnp.einsum("sd,qdf->sqf", row_block, up_all, preferred_element_type=jnp.float32)
    activated = (jax.nn.silu(gate_part) * up_part).astype(jnp.bfloat16)
    expert_rows = jnp.einsum(
        "sqf,qfd->sd", activated, down_all, preferred_element_type=jnp.float32
    ).astype(jnp.bfloat16)
    returned = lax.all_to_all(
        expert_rows.reshape(peer_count, slots, model_width),
        "expert",
        split_axis=0,
        concat_axis=0,
        tiled=True,
    ).reshape(peer_count * slots, model_width)

    spread = jnp.where(taken, jnp.repeat(gate_weights, slots, axis=1), 0.0)
    spread_high = spread.astype(jnp.bfloat16)
    spread_low = (spread - spread_high.astype(jnp.float32)).astype(jnp.bfloat16)
    mixture = jnp.dot(spread_high, returned, preferred_element_type=jnp.float32) + jnp.dot(
        spread_low, returned, preferred_element_type=jnp.float32
    )
    mixture = lax.psum_scatter(mixture, "tensor", scatter_dimension=1, tiled=True)
    residual_mine = lax.dynamic_slice_in_dim(residual, feature_first, feature_share, 1)
    total_mine = residual_mine.astype(jnp.float32) + mixture
    squares = lax.psum(jnp.sum(total_mine * total_mine, axis=-1), "tensor")
    inverse_rms = lax.rsqrt(squares / model_width + epsilon)[:, None]
    normalized = (total_mine * inverse_rms * final_gain.astype(jnp.float32)).astype(jnp.bfloat16)
    picks = (asked.reshape(rows_dev)[:, None] == jnp.arange(rows_dev)[None, :]).astype(jnp.bfloat16)
    packed = jnp.dot(picks, normalized, preferred_element_type=jnp.float32).astype(jnp.bfloat16)
    arrived = lax.all_to_all(
        packed.reshape(peer_count, peer_rows, feature_share),
        "expert",
        split_axis=0,
        concat_axis=0,
        tiled=True,
    ).reshape(rows_dev, feature_share)
    return jnp.dot(
        places.astype(jnp.bfloat16), arrived, preferred_element_type=jnp.float32
    ).astype(jnp.bfloat16)


def solution(mesh):
    placed = (
        P("expert", "tensor"),
        P("tensor", None),
        P("expert", None),
        P(),
        P(),
        P("expert", None),
        P("expert", None, "tensor"),
        P("expert", None, "tensor"),
        P("expert", "tensor", None),
        P("tensor"),
        P("expert"),
    )
    return jax.shard_map(
        on_device, mesh=mesh, in_specs=placed, out_specs=P("expert", "tensor"), check_vma=False
    )
```

time: 755 us -> 365 us (0.48)
  waiting for transfers between devices: 394 us -> 205 us
  blocking collectives: 228 us -> 93.1 us
  local copies, waits for them, and re-layouts: 46.1 us -> 3.23 us
  other arithmetic: 34.4 us -> 3.63 us
  matrix products: 15.7 us -> 28.2 us
    all_to_all x1, waiting for transfers between devices: 357 us -> 49.1 us  [on_device(): lax.all_to_all(expert_rows.reshape(peer_count, slots, model_width), 'expe...]
    all_to_all x1, blocking collectives: 197 us -> 61.6 us  [on_device(): lax.all_to_all(outgoing, 'expert', split_axis=0, concat_axis=0, tiled=True)]
    all_gather x0 -> x3, waiting for transfers between devices: none -> 90.8 us  [the longest x1 53 us: on_device(): down_all = lax.all_gather(w_down[0], 'tensor')]
    gather x9 -> x0, local copies, waits for them, and re-layouts: 35.3 us -> none  [the longest x1 14.9 us: on_device(): flat_back[slot_index].reshape(rows_dev, top_count, returned.shape[3])]
    psum x1, waiting for transfers between devices: 28 us -> 51.1 us  [on_device(): attention = lax.psum(head_term, 'tensor')]
    another operation x2 -> x0, other arithmetic: 18 us -> none
    dot_general x3 -> x8, matrix products: 13 us -> 25.4 us  [the longest x1 10.8 us: on_device(): jnp.einsum('sqf,qfd->sd', activated, down_all, preferred_element_type=jnp...]
    all_to_all x1, starting transfers between devices: 14.6 us -> 7.02 us  [on_device(): lax.all_to_all(wanted, 'expert', split_axis=0, concat_axis=0, tiled=True)]
  transfers between devices with their start and end apart: 4 -> 7, of which waited for: 3 -> 6; matrix products, arithmetic and copies ran while one was open for 5% -> 3% of each run, Pallas kernels for 0% -> 0%
where the time goes in v1:
time: 365 us
  waiting for transfers between devices  205 us (56%)
  blocking collectives  93.1 us (26%)
  matrix products  28.2 us (8%)
  starting transfers between devices  18.2 us (5%)
  between operations  13.3 us (4%)
    all_to_all x1, blocking collectives, on_device(): lax.all_to_all(outgoing, 'expert', split_axis=0, concat_axis=0, tiled=True)  61.6 us
    all_gather x1, waiting for transfers between devices, on_device(): down_all = lax.all_gather(w_down[0], 'tensor')  53 us
    psum x1, waiting for transfers between devices, on_device(): attention = lax.psum(head_term, 'tensor')  51.1 us
    all_to_all x1, waiting for transfers between devices, on_device(): lax.all_to_all(expert_rows.reshape(peer_count, slots, model_width), 'expe...  49.1 us
    all_gather x1, waiting for transfers between devices, on_device(): gate_all = lax.all_gather(w_gate[0], 'tensor')  37.8 us
    all_to_all x1, blocking collectives, on_device(): lax.all_to_all(packed.reshape(peer_count, peer_rows, feature_share), 'exp...  24.9 us
    all_to_all x1, starting transfers between devices, on_device(): lax.all_to_all(expert_rows.reshape(peer_count, slots, model_width), 'expe...  11 us
    dot_general x1, matrix products, on_device(): jnp.einsum('sqf,qfd->sd', activated, down_all, preferred_element_type=jnp...  10.8 us
  transfers between devices with their start and end apart: 7, of which 6 were waited for; matrix products, arithmetic and copies ran while one was open for 3% of the time, Pallas kernels for 0%

profile of v1, /device:TPU:1, one launch (start us, length us, event | category | flops | bytes accessed | tf_op | source)
XLA Modules:
  0.0 364.6 jit_solution(6896909703667646671)
XLA Ops:
  6.5 0.0 copy-start
  6.5 0.0 all-reduce.2.cloned.1.call-start
  6.5 1.6 copy-done
  8.1 2.3 fusion.47
  10.5 0.0 all-reduce.2.cloned.1.call-update
  10.5 0.0 all-gather.6.cloned.1.call-start
  10.5 0.7 all-gather.6.cloned.1.call-update
  11.2 0.0 all-gather.4.cloned.1.call-start
  11.3 0.7 all-gather.4.cloned.1.call-update
  12.0 0.0 all-gather.8.cloned.1.call-start
  12.0 0.5 all-gather.8.cloned.1.call-update
  12.6 0.1 eq.94
  12.7 0.0 copy-done.3
  12.7 0.1 fusion.10
  12.9 51.1 %all-reduce.2.cloned.1.call-done = f32[128,2048]{1,0:T(8,128)} async-done(((f32[128,2048]{1,0:T(8,128)}), f32[128,2048]{1,0:T(8,128)}) %all-reduce.2.cloned.1.call-update) | async-done | bytes 1048592 | tf_op jit(solution)/shard_map/psum | solution.py:57
  63.9 1.5 fusion.11
  65.4 0.8 fusion
  66.2 61.6 %all_to_all.24 = bf16[64,8,2048]{2,1,0:T(8,128)(2,1)} all-to-all(bf16[64,8,2048]{2,1,0:T(8,128)(2,1)S(1)} %fusion), channel_id=1, replica_groups=mesh['tensor'=4,'expert'=64] {'expert'}, dimensions={0} | all-to-all | bytes 4194304 | tf_op jit(solution)/shard_map/all_to_all | solution.py:77
  127.9 6.5 %fusion.3 = f32[512,4,256]{2,0,1:T(8,128)} fusion(bf16[4,2048,256]{2,1,0:T(8,128)(2,1)} %all-gather.6.cloned.1.call-done, bf16[64,8,2048]{2,1,0:T(8,128)(2,1)} %all_to_all.24), kind=kOutput, calls=%fused_computation.7 | convolution fusion | flops 2147483648 | bytes 8388608 | tf_op jit(solution)/shard_map/sd,qdf->sqf/dot_general | solution.py:81
  134.4 37.8 %all-gather.4.cloned.1.call-done = bf16[4,2048,256]{2,1,0:T(8,128)(2,1)} async-done(((bf16[1,2048,256]{2,1,0:T(8,128)(2,1)}), bf16[4,2048,256]{2,1,0:T(8,128)(2,1)}) %all-gather.4.cloned.1.call-update) | async-done | bytes 4194320 | tf_op jit(solution)/shard_map/all_gather | solution.py:52
  172.2 53.0 %all-gather.8.cloned.1.call-done = bf16[4,256,2048]{2,1,0:T(8,128)(2,1)} async-done(((bf16[1,256,2048]{2,1,0:T(8,128)(2,1)}), bf16[4,256,2048]{2,1,0:T(8,128)(2,1)}) %all-gather.8.cloned.1.call-update) | async-done | bytes 4194320 | tf_op jit(solution)/shard_map/all_gather | solution.py:54
  225.2 10.8 %fusion.1 = bf16[64,8,2048]{2,1,0:T(8,128)(2,1)} fusion(bf16[4,256,2048]{2,1,0:T(8,128)(2,1)} %all-gather.8.cloned.1.call-done, f32[512,4,256]{2,0,1:T(8,128)} %fusion.3, bf16[4,2048,256]{2,1,0:T(8,128)(2,1)} %all-gather.4.cloned.1.call-done, bf16[64,8,2048]{2,1,0:T(8,128)(2,1)} %all_to_all.24), kind=kOutput, calls=%fused_computation.3 | convolution fusion | flops 4299161600 | bytes 14680064 | tf_op jit(solution)/shard_map/sqf,qfd->sd/dot_general | solution.py:83
  235.9 11.0 %all-to-all-start.2 = ((bf16[64,8,2048]{2,1,0:T(8,128)(2,1)}), bf16[64,8,2048]{2,1,0:T(8,128)(2,1)}, u32[]{:S(2)}, u32[]{:S(2)}) async-start(bf16[64,8,2048]{2,1,0:T(8,128)(2,1)} %fusion.1), calls=%async_computation.2 | async-start | bytes 4194304 | tf_op jit(solution)/shard_map/all_to_all | solution.py:86
  247.0 0.0 reduce-scatter.2.cloned.1.call-start
  247.0 0.4 fusion.46
  247.4 49.1 %all-to-all-done.2 = bf16[64,8,2048]{2,1,0:T(8,128)(2,1)} async-done(((bf16[64,8,2048]{2,1,0:T(8,128)(2,1)}), bf16[64,8,2048]{2,1,0:T(8,128)(2,1)}, u32[]{:S(2)}, u32[]{:S(2)}) %all-to-all-start.2) | async-done | bytes 2097184 | tf_op jit(solution)/shard_map/all_to_all | solution.py:86
  296.5 2.1 convolution_bitcast_fusion
  298.6 0.0 copy-start.6
  298.6 0.0 copy-start.4
  298.7 3.1 fusion.2
  301.7 0.0 reduce-scatter.2.cloned.1.call-update
  301.8 0.2 convert_reduce_fusion
  302.0 0.1 select_reduce_fusion
  302.1 0.8 all_to_all.15
  302.9 7.0 %all-to-all-start = ((s32[64,1,2]{2,1,0:T(1,128)}), s32[64,1,2]{2,1,0:T(1,128)S(1)}, u32[]{:S(2)}, u32[]{:S(2)}) async-start(s32[64,1,2]{2,1,0:T(1,128)} %bitcast), calls=%async_computation | async-start | bytes 65536 | tf_op jit(solution)/shard_map/all_to_all | solution.py:50
  309.9 0.0 copy-done.4
  309.9 9.3 %all-to-all-done = s32[64,1,2]{2,1,0:T(1,128)S(1)} async-done(((s32[64,1,2]{2,1,0:T(1,128)}), s32[64,1,2]{2,1,0:T(1,128)S(1)}, u32[]{:S(2)}, u32[]{:S(2)}) %all-to-all-start) | async-done | bytes 544 | tf_op jit(solution)/shard_map/all_to_all | solution.py:50
  319.2 0.5 broadcast.64
  319.7 0.7 reduce.3
  320.4 0.1 eq.83
  320.6 2.7 reduce-scatter.2.cloned.1.call-done
  323.3 1.1 multiply_reduce_fusion
  324.4 6.6 %psum.15 = f32[128]{0:T(128)S(1)} all-reduce(f32[128]{0:T(128)S(1)} %multiply_reduce_fusion), channel_id=1, replica_groups=mesh['tensor'=4,'expert'=64] {'tensor'}, use_global_device_ids=true, to_apply=%region_8.9 | all-reduce | flops 128 | bytes 1024 | tf_op jit(solution)/shard_map/psum | solution.py:103
  331.0 1.2 convolution_convert_fusion.2
  332.2 0.1 reshape.61
  332.3 24.9 %all_to_all.25 = bf16[64,2,512]{2,1,0:T(2,128)(2,1)S(1)} all-to-all(bf16[64,2,512]{2,1,0:T(2,128)(2,1)S(1)} %reshape.61), channel_id=1, replica_groups=mesh['tensor'=4,'expert'=64] {'expert'}, dimensions={0} | all-to-all | bytes 262144 | tf_op jit(solution)/shard_map/all_to_all | solution.py:108
  357.2 0.1 reshape.62
  357.2 0.9 convolution_convert_fusion.1
  (18 shorter events, 0.1 us)
Async XLA Ops:
  6.5 1.6 copy-start
  6.5 57.4 %all-reduce.2.cloned.1.call-start = ((), (), s32[]{:S(2)}) async-start(), calls=%async_computation.5 | async-start | bytes 2097152 | tf_op jit(solution)/shard_map/psum | solution.py:57
  10.4 2.1 copy-start.2
  10.5 2.2 copy-start.3
  10.5 53.5 %copy-start.1 = (bf16[128,2048]{1,0:T(8,128)(2,1)S(1)}, bf16[128,2048]{1,0:T(8,128)(2,1)}, u32[]{:S(2)}) copy-start(bf16[128,2048]{1,0:T(8,128)(2,1)} %param.13) | copy-start | bytes 1572868
  10.5 117.4 %all-gather.6.cloned.1.call-start = ((), (), s32[]{:S(2)}) async-start(), calls=%async_computation.7 | async-start | bytes 5242880 | tf_op jit(solution)/shard_map/all_gather | solution.py:53
  11.2 160.9 %all-gather.4.cloned.1.call-start = ((), (), s32[]{:S(2)}) async-start(), calls=%async_computation.6 | async-start | bytes 5242880 | tf_op jit(solution)/shard_map/all_gather | solution.py:52
  12.0 213.2 %all-gather.8.cloned.1.call-start = ((), (), s32[]{:S(2)}) async-start(), calls=%async_computation.8 | async-start | bytes 5242880 | tf_op jit(solution)/shard_map/all_gather | solution.py:54
  235.9 11.1 %copy-start.5 = (bf16[2048,64]{0,1:T(8,128)(2,1)S(1)}, bf16[2048,64]{0,1:T(8,128)(2,1)}, u32[]{:S(2)}) copy-start(bf16[2048,64]{0,1:T(8,128)(2,1)} %param.15) | copy-start | bytes 786436
  235.9 60.6 %all-to-all-start.2 = ((bf16[64,8,2048]{2,1,0:T(8,128)(2,1)}), bf16[64,8,2048]{2,1,0:T(8,128)(2,1)}, u32[]{:S(2)}, u32[]{:S(2)}) async-start(bf16[64,8,2048]{2,1,0:T(8,128)(2,1)} %fusion.1), calls=%async_computation.2 | async-start | bytes 4194304 | tf_op jit(solution)/shard_map/all_to_all | solution.py:86
  247.0 76.4 %reduce-scatter.2.cloned.1.call-start = ((), (), s32[]{:S(2)}) async-start(), calls=%async_computation.9 | async-start | bytes 1310720 | tf_op jit(solution)/shard_map/reduce_scatter | solution.py:100
  298.6 3.1 copy-start.6
  298.6 11.2 %copy-start.4 = (bf16[512]{0:T(512)(128)(2,1)S(1)}, bf16[512]{0:T(512)(128)(2,1)}, u32[]{:S(2)}) copy-start(bf16[512]{0:T(512)(128)(2,1)} %param.20) | copy-start | bytes 3076
  302.9 16.3 %all-to-all-start = ((s32[64,1,2]{2,1,0:T(1,128)}), s32[64,1,2]{2,1,0:T(1,128)S(1)}, u32[]{:S(2)}, u32[]{:S(2)}) async-start(s32[64,1,2]{2,1,0:T(1,128)} %bitcast), calls=%async_computation | async-start | bytes 65536 | tf_op jit(solution)/shard_map/all_to_all | solution.py:50
Sparse Core Ops, SparseCore 0:
  10.6 53.2 all-reduce.1
  65.9 53.0 all-gather.5
  121.0 51.1 all-gather.3
  174.0 51.1 all-gather.7
  301.9 21.3 reduce-scatter.1

commit v2 on v0

v2 whole, which is shorter than its diff:
```python
import functools

import jax
import jax.numpy as jnp
from jax import lax
from jax.experimental import pallas as pl
from jax.experimental.pallas import tpu as pltpu
from jax.sharding import PartitionSpec as P

epsilon = 1e-06
BF = jnp.bfloat16
F32 = jnp.float32
VMEM = pltpu.VMEM
DMA = pltpu.SemaphoreType.DMA


def dot(a, b):
    return jnp.dot(a, b, preferred_element_type=F32)


def iota(shape, dim):
    return lax.broadcasted_iota(jnp.int32, shape, dim)


def layer(
    planes,
    peers,
    attn_ref,
    proj_ref,
    hidden_ref,
    gain_ref,
    router_ref,
    routes_ref,
    gate_hbm,
    up_hbm,
    down_hbm,
    last_gain_ref,
    source_ref,
    out_ref,
    part,
    att_send,
    att_recv,
    res,
    normed,
    gates,
    ups,
    downs,
    ask_send,
    ask_recv,
    slot_send,
    slot_recv,
    rows_in,
    acts,
    back_send,
    back_recv,
    mix_send,
    mix_recv,
    mix_own,
    total,
    sq_send,
    sq_recv,
    pack_send,
    pack_recv,
    high,
    low,
    own_sem,
    att_s,
    att_r,
    res_s,
    res_r,
    ask_s,
    ask_r,
    slot_s,
    slot_r,
    w_s,
    w_r,
    d_s,
    d_r,
    back_s,
    back_r,
    mix_s,
    mix_r,
    sq_s,
    sq_r,
    pack_s,
    pack_r,
):
    x = lax.axis_index("tensor")
    me = lax.axis_index("expert")
    rows, share = attn_ref.shape
    width = planes * share
    slots = slot_send.shape[1]
    all_slots = peers * slots
    hidden_units = gate_hbm.shape[2]
    right = lax.rem(x + 1, planes)
    left = lax.rem(x + planes - 1, planes)

    def to_plane(src, dst, send, recv, plane):
        return pltpu.make_async_remote_copy(
            src_ref=src, dst_ref=dst, send_sem=send, recv_sem=recv, device_id={"tensor": plane}
        )

    def to_peer(src, dst, send, recv, peer):
        return pltpu.make_async_remote_copy(
            src_ref=src, dst_ref=dst, send_sem=send, recv_sem=recv, device_id={"expert": peer}
        )

    def peer_at(step):
        return lax.rem(me + step, peers)

    own = [
        pltpu.make_async_copy(gate_hbm.at[0], gates.at[0], own_sem.at[0]),
        pltpu.make_async_copy(up_hbm.at[0], ups.at[0], own_sem.at[1]),
    ]
    for j in range(planes):
        own.append(
            pltpu.make_async_copy(
                down_hbm.at[0, :, pl.ds(j * share, share)], downs.at[0, j], own_sem.at[2 + j]
            )
        )
    for copy in own:
        copy.start()

    barrier = pltpu.get_barrier_semaphore()
    for d in range(1, planes):
        pl.semaphore_signal(barrier, inc=1, device_id={"tensor": lax.rem(x + d, planes)})

    @pl.loop(1, peers)
    def _(step):
        pl.semaphore_signal(barrier, inc=1, device_id={"expert": peer_at(step)})

    ask_send[...] = jnp.broadcast_to(source_ref[...], ask_send.shape)
    for j in range(planes):
        part[j] = dot(attn_ref[...], proj_ref[:, j * share : (j + 1) * share])
    for d in range(1, planes):
        att_send[d - 1] = part[lax.rem(x + d, planes)].astype(BF)

    pl.semaphore_wait(barrier, planes - 1 + peers - 1)

    att = [
        to_plane(
            att_send.at[d - 1],
            att_recv.at[d - 1],
            att_s.at[d - 1],
            att_r.at[d - 1],
            lax.rem(x + d, planes),
        )
        for d in range(1, planes)
    ]
    for copy in att:
        copy.start()

    @pl.loop(1, peers)
    def _(step):
        to_peer(ask_send, ask_recv.at[me], ask_s, ask_r, peer_at(step)).start()

    for copy in att:
        copy.wait_recv()
    mine = pl.ds(pl.multiple_of(x * share, share), share)
    attention = part[x]
    for d in range(planes - 1):
        attention = attention + att_recv[d].astype(F32)
    res[x] = (hidden_ref[:, mine].astype(F32) + attention).astype(BF)
    spread_res = [
        to_plane(res.at[x], res.at[x], res_s.at[d - 1], res_r.at[d - 1], lax.rem(x + d, planes))
        for d in range(1, planes)
    ]
    for copy in spread_res:
        copy.start()

    gate_r = to_plane(gate_hbm.at[0], gates.at[1], w_s.at[0], w_r.at[0], right)
    up_r = to_plane(up_hbm.at[0], ups.at[1], w_s.at[1], w_r.at[1], right)
    up_l = to_plane(up_hbm.at[0], ups.at[2], w_s.at[2], w_r.at[2], left)
    gate_l = to_plane(gate_hbm.at[0], gates.at[2], w_s.at[3], w_r.at[3], left)
    gate_on = to_plane(gates.at[1], gates.at[3], w_s.at[4], w_r.at[4], right)
    up_on = to_plane(ups.at[2], ups.at[3], w_s.at[5], w_r.at[5], left)
    gate_r.start()
    up_l.start()
    up_r.start()
    gate_l.start()

    for copy in spread_res:
        copy.wait_recv()
    square = jnp.zeros((rows, 1), F32)
    for j in range(planes):
        floats = res[j].astype(F32)
        square = square + jnp.sum(floats * floats, axis=1, keepdims=True)
    inverse = lax.rsqrt(square / width + epsilon)
    experts = peers
    logits = jnp.zeros((rows, experts), F32)
    for j in range(planes):
        cols = slice(j * share, (j + 1) * share)
        scaled = (res[j].astype(F32) * inverse * gain_ref[:, cols].astype(F32)).astype(BF)
        normed[j] = scaled
        logits = logits + dot(scaled, router_ref[cols, :])
    named = jnp.zeros((rows, experts), jnp.bool_)
    which = iota((rows, experts), 1)
    for k in range(routes_ref.shape[1]):
        named = named | (routes_ref[:, k : k + 1] == which)
    named_f = jnp.where(named, 1.0, 0.0).astype(F32)
    powers = jnp.where(named, jnp.exp(logits), 0.0)
    weights = powers / jnp.sum(powers, axis=1, keepdims=True)
    before = jnp.where(iota((rows, rows), 1) < iota((rows, rows), 0), 1.0, 0.0).astype(BF)
    rank = dot(before, named_f.astype(BF))
    wide = jnp.where(
        iota((experts, all_slots), 1) // slots == iota((experts, all_slots), 0), 1.0, 0.0
    ).astype(BF)
    wide_rank = dot(rank.astype(BF), wide)
    wide_named = dot(named_f.astype(BF), wide)
    turn = (iota((rows, all_slots), 1) % slots + x * slots).astype(F32)
    taken = (wide_named > 0.5) & (wide_rank == turn)
    weights_high = weights.astype(BF)
    weights_low = (weights - weights_high.astype(F32)).astype(BF)
    high[...] = jnp.where(taken, dot(weights_high, wide), 0.0).astype(BF)
    low[...] = jnp.where(taken, dot(weights_low, wide), 0.0).astype(BF)
    pick = jnp.transpose(jnp.where(taken, 1.0, 0.0).astype(F32)).astype(BF)
    for j in range(planes):
        chosen = dot(pick, normed[j]).astype(BF)
        slot_send[:, :, j * share : (j + 1) * share] = chosen.reshape(peers, slots, share)

    @pl.loop(1, peers)
    def _(step):
        peer = peer_at(step)
        to_peer(slot_send.at[peer], slot_recv.at[me], slot_s, slot_r, peer).start()

    own_slot = pltpu.make_async_copy(slot_send.at[me], slot_recv.at[me], own_sem.at[2 + planes])
    own_slot.start()

    gate_r.wait_recv()
    gate_on.start()
    up_l.wait_recv()
    up_on.start()

    half = hidden_units // 2
    down_r, down_l, on_r, on_l = [], [], [], []
    for j in range(planes):
        cols = pl.ds(j * share, share)
        down_r.append(
            to_plane(down_hbm.at[0, :, cols], downs.at[1, j], d_s.at[0, j], d_r.at[0, j], right)
        )
        down_l.append(
            to_plane(down_hbm.at[0, :, cols], downs.at[2, j], d_s.at[1, j], d_r.at[1, j], left)
        )
        top, bottom = pl.ds(0, half), pl.ds(half, half)
        on_r.append(
            to_plane(
                downs.at[1, j, top], downs.at[3, j, top], d_s.at[2, j], d_r.at[2, j], right
            )
        )
        on_l.append(
            to_plane(
                downs.at[2, j, bottom], downs.at[3, j, bottom], d_s.at[3, j], d_r.at[3, j], left
            )
        )
    for j in range(2):
        down_r[j].start()
        down_l[j].start()

    everyone = pl.ds(0, peers - 1)
    to_peer(slot_send.at[everyone], slot_recv.at[everyone], slot_s, slot_r, me).wait_recv()
    own_slot.wait()
    tiles = 4
    tile_peers = peers // tiles
    tile_rows = tile_peers * slots
    for t in range(tiles):
        rows_in[t * tile_rows : (t + 1) * tile_rows] = slot_recv[
            t * tile_peers : (t + 1) * tile_peers
        ].reshape(tile_rows, width)

    def activate(q):
        gate_part = dot(rows_in[...], gates[q])
        up_part = dot(rows_in[...], ups[q])
        acts[q] = (gate_part / (1.0 + jnp.exp(-gate_part)) * up_part).astype(BF)

    own[0].wait()
    own[1].wait()
    activate(0)
    up_r.wait_recv()
    activate(1)
    gate_l.wait_recv()
    activate(2)

    for copy in own[2:]:
        copy.wait()
    down_r[0].wait_recv()
    on_r[0].start()
    down_l[0].wait_recv()
    on_l[0].start()
    for j in range(2, planes):
        down_r[j].start()
        down_l[j].start()

    gate_on.wait_recv()
    up_on.wait_recv()
    activate(3)

    def combine(j):
        to_peer(
            back_send.at[j, everyone], back_recv.at[j, everyone], back_s.at[j], back_r.at[j], me
        ).wait_recv()
        back = back_recv[j].reshape(all_slots, share)
        mixed = dot(high[...], back) + dot(low[...], back)
        mix_send[j] = mixed.astype(BF)

        @pl.when(x == j)
        def _():
            mix_own[...] = mixed

        @pl.when(x != j)
        def _():
            to_plane(mix_send.at[j], mix_recv.at[x], mix_s, mix_r, j).start()

    for j in range(planes):
        if j + 1 < planes:
            down_r[j + 1].wait_recv()
            on_r[j + 1].start()
            down_l[j + 1].wait_recv()
            on_l[j + 1].start()
        on_r[j].wait_recv()
        on_l[j].wait_recv()
        product = dot(acts[0], downs[0, j])
        for q in range(1, planes):
            product = product + dot(acts[q], downs[q, j])
        back_send[j] = product.astype(BF).reshape(peers, slots, share)
        back_recv[j, me] = back_send[j, me]

        @pl.loop(1, peers)
        def _(step):
            peer = peer_at(step)
            to_peer(
                back_send.at[j, peer], back_recv.at[j, me], back_s.at[j], back_r.at[j], peer
            ).start()

        if j >= 1:
            combine(j - 1)
    combine(planes - 1)

    three = pl.ds(0, planes - 1)
    to_plane(mix_send.at[three], mix_recv.at[three], mix_s, mix_r, x).wait_recv()
    whole = mix_own[...] + res[x].astype(F32)
    for j in range(planes):
        whole = whole + jnp.where(x == j, 0.0, mix_recv[j].astype(F32))
    total[...] = whole
    squares = jnp.zeros((rows, 128), F32)
    for c in range(share // 128):
        piece = whole[:, c * 128 : (c + 1) * 128]
        squares = squares + piece * piece
    row_sum = jnp.sum(jnp.transpose(squares), axis=0, keepdims=True)
    sq_send[...] = jnp.broadcast_to(row_sum, sq_send.shape)
    sq = [
        to_plane(sq_send, sq_recv.at[d - 1], sq_s.at[d - 1], sq_r.at[d - 1], lax.rem(x + d, planes))
        for d in range(1, planes)
    ]
    for copy in sq:
        copy.start()

    to_peer(ask_recv.at[everyone], ask_recv.at[everyone], ask_s, ask_r, me).wait_recv()
    ask_recv[me] = ask_send[...]
    asked = ask_recv[...].reshape(peers * 8, rows)
    lanes = iota((peers * 8, rows), 1)
    ours = asked // rows == me
    first = jnp.min(jnp.where(ours, lanes, rows), axis=1, keepdims=True)
    second = jnp.max(jnp.where(ours, lanes, -1), axis=1, keepdims=True)
    line = iota((peers * 8, 1), 0) % 8
    request = jnp.where(line < 4, first, second)
    local = jnp.sum(jnp.where(lanes == request, asked % rows, 0), axis=1, keepdims=True)
    wanted = lanes == local

    for copy in sq:
        copy.wait_recv()
    sums = sq_send[...]
    for d in range(planes - 1):
        sums = sums + sq_recv[d]
    column = jnp.transpose(jnp.broadcast_to(sums[0:1], (rows, rows)))[:, 0:1]
    scale = lax.rsqrt(column / width + epsilon)
    result = (total[...] * scale * last_gain_ref[...].astype(F32)).astype(BF)
    packed = jnp.zeros((peers * 8, 128), F32)
    for c in range(4):
        chooser = jnp.where(wanted & (line % 4 == c), 1.0, 0.0).astype(BF)
        packed = packed + dot(chooser, result[:, c * 128 : (c + 1) * 128])
    pack_send[...] = packed.astype(BF).reshape(peers, 8, 128)
    pack_recv[me] = pack_send[me]

    @pl.loop(1, peers)
    def _(step):
        peer = peer_at(step)
        to_peer(pack_send.at[peer], pack_recv.at[me], pack_s, pack_r, peer).start()

    asks = jnp.broadcast_to(source_ref[...], (rows, rows))
    asks_down = jnp.transpose(asks.astype(F32)).astype(jnp.int32)
    same = (asks // rows == asks_down // rows) & (iota((rows, rows), 1) < iota((rows, rows), 0))
    later = jnp.max(jnp.where(same, 1, 0), axis=1, keepdims=True)
    place = (asks_down[:, 0:1] // rows) * 8 + later * 4
    at = iota((rows, peers * 8), 1)
    to_peer(pack_send.at[everyone], pack_recv.at[everyone], pack_s, pack_r, me).wait_recv()
    landed = pack_recv[...].reshape(peers * 8, 128)
    for c in range(4):
        chooser = jnp.where(at == place + c, 1.0, 0.0).astype(BF)
        out_ref[:, c * 128 : (c + 1) * 128] = dot(chooser, landed).astype(BF)

    for copy in (
        att + spread_res + [gate_r, up_r, up_l, gate_l, gate_on, up_on]
        + down_r + down_l + on_r + on_l + sq
    ):
        copy.wait_send()

    @pl.loop(1, peers)
    def _(step):
        to_peer(ask_send, ask_recv.at[me], ask_s, ask_r, me).wait_send()

    to_peer(slot_send.at[everyone], slot_recv.at[everyone], slot_s, slot_r, me).wait_send()
    for j in range(planes):
        to_peer(
            back_send.at[j, everyone], back_recv.at[j, everyone], back_s.at[j], back_r.at[j], me
        ).wait_send()
    to_plane(mix_send.at[three], mix_recv.at[three], mix_s, mix_r, x).wait_send()
    to_peer(pack_send.at[everyone], pack_recv.at[everyone], pack_s, pack_r, me).wait_send()


def solution(mesh):
    planes, peers = mesh.shape["tensor"], mesh.shape["expert"]

    def on_device(
        attn_out,
        out_proj,
        hidden_in,
        norm_gain,
        router,
        routes,
        w_gate,
        w_up,
        w_down,
        final_gain,
        source,
    ):
        rows, width = hidden_in.shape
        share = width // planes
        top = routes.shape[1]
        slots = min(rows, 2 * rows * top // peers) // planes
        units = w_gate.shape[2]
        local = pl.BlockSpec(memory_space=pltpu.VMEM)
        remote = pl.BlockSpec(memory_space=pl.ANY)
        return pl.pallas_call(
            functools.partial(layer, planes, peers),
            out_shape=jax.ShapeDtypeStruct((rows, share), BF),
            in_specs=[local] * 6 + [remote] * 3 + [local] * 2,
            out_specs=local,
            scratch_shapes=[
                VMEM((planes, rows, share), F32),
                VMEM((planes - 1, rows, share), BF),
                VMEM((planes - 1, rows, share), BF),
                VMEM((planes, rows, share), BF),
                VMEM((planes, rows, share), BF),
                VMEM((planes, width, units), BF),
                VMEM((planes, width, units), BF),
                VMEM((planes, planes, units, share), BF),
                VMEM((8, rows), jnp.int32),
                VMEM((peers, 8, rows), jnp.int32),
                VMEM((peers, slots, width), BF),
                VMEM((peers, slots, width), BF),
                VMEM((peers * slots, width), BF),
                VMEM((planes, peers * slots, units), BF),
                VMEM((planes, peers, slots, share), BF),
                VMEM((planes, peers, slots, share), BF),
                VMEM((planes, rows, share), BF),
                VMEM((planes, rows, share), BF),
                VMEM((rows, share), F32),
                VMEM((rows, share), F32),
                VMEM((8, rows), F32),
                VMEM((planes - 1, 8, rows), F32),
                VMEM((peers, 8, 128), BF),
                VMEM((peers, 8, 128), BF),
                VMEM((rows, peers * slots), BF),
                VMEM((rows, peers * slots), BF),
                DMA((3 + planes,)),
                DMA((planes - 1,)),
                DMA((planes - 1,)),
                DMA((planes - 1,)),
                DMA((planes - 1,)),
                DMA,
                DMA,
                DMA,
                DMA,
                DMA((6,)),
                DMA((6,)),
                DMA((4, planes)),
                DMA((4, planes)),
                DMA((planes,)),
                DMA((planes,)),
                DMA,
                DMA,
                DMA((planes - 1,)),
                DMA((planes - 1,)),
                DMA,
                DMA,
            ],
            compiler_params=pltpu.CompilerParams(
                collective_id=0, has_side_effects=True, vmem_limit_bytes=56 * 1024 * 1024
            ),
        )(
            attn_out,
            out_proj,
            hidden_in,
            norm_gain.reshape(1, width),
            router,
            routes,
            w_gate,
            w_up,
            w_down,
            final_gain.reshape(1, share),
            source.reshape(1, rows),
        )

    placed = (
        P("expert", "tensor"),
        P("tensor", None),
        P("expert", None),
        P(),
        P(),
        P("expert", None),
        P("expert", None, "tensor"),
        P("expert", None, "tensor"),
        P("expert", "tensor", None),
        P("tensor"),
        P("expert"),
    )
    return jax.shard_map(
        on_device, mesh=mesh, in_specs=placed, out_specs=P("expert", "tensor"), check_vma=False
    )
```

time: 755 us -> 192 us (0.25)
  waiting for transfers between devices: 394 us -> 0 us
  blocking collectives: 228 us -> 0 us
  Pallas kernels: 0 us -> 185 us
  local copies, waits for them, and re-layouts: 46.1 us -> 7.46 us
  other arithmetic: 34.4 us -> 0 us
  starting transfers between devices: 22.3 us -> 0 us
  matrix products: 15.7 us -> 0 us
  between operations: 13.7 us -> 0.01 us
    all_to_all x2 -> x0, waiting for transfers between devices: 366 us -> none  [the longest x1 357 us: on_device(): lax.all_to_all(partial_value, 'expert', split_axis=0, concat_axis=0, tile...]
    all_to_all x2 -> x0, blocking collectives: 220 us -> none  [the longest x1 197 us: on_device(): lax.all_to_all(outgoing, 'expert', split_axis=0, concat_axis=0, tiled=True)]
    pallas_call x0 -> x1, Pallas kernels: none -> 185 us  [on_device(): pl.pallas_call(functools.partial(layer, planes, peers), out_shape=jax.Sha...]
    gather x9 -> x0, local copies, waits for them, and re-layouts: 35.3 us -> none  [the longest x1 14.9 us: on_device(): flat_back[slot_index].reshape(rows_dev, top_count, returned.shape[3])]
    psum x1 -> x0, waiting for transfers between devices: 28 us -> none  [on_device(): attention = lax.psum(head_term, 'tensor')]
    all_to_all x2 -> x0, starting transfers between devices: 22.3 us -> none  [the longest x1 14.6 us: on_device(): lax.all_to_all(wanted, 'expert', split_axis=0, concat_axis=0, tiled=True)]
    another operation x2 -> x0, other arithmetic: 18 us -> none
    dot_general x5 -> x0, matrix products: 15.7 us -> none  [the longest x1 8.06 us: swiglu_rows(): return jnp.dot(activated, down_matrix, preferred_element_type=jnp.float32)]
  transfers between devices with their start and end apart: 4 -> 0, of which waited for: 3 -> 0; matrix products, arithmetic and copies ran while one was open for 5% -> 0% of each run, Pallas kernels for 0% -> 0%
where the time goes in v2:
time: 192 us
  Pallas kernels  185 us (96%)
  local copies, waits for them, and re-layouts  7.46 us (4%)
    pallas_call x1, Pallas kernels, on_device(): pl.pallas_call(functools.partial(layer, planes, peers), out_shape=jax.Sha...  185 us
    unnamed x3, local copies, waits for them, and re-layouts  4.93 us

profile of v2, /device:TPU:1, one launch (start us, length us, event | category | flops | bytes accessed | tf_op | source)
XLA Modules:
  0.0 192.0 jit_solution(11974542798228717805)
XLA Ops:
  0.0 1.3 reshape.10.last_gain_ref
  1.3 1.3 reshape.9.gain_ref
  2.5 1.4 copy.13.routes_ref
  3.9 1.9 %copy.12.router_ref = bf16[2048,64]{1,0:T(8,128)(2,1)} copy(bf16[2048,64]{0,1:T(8,128)(2,1)} %param.15) | data formatting | bytes 524288 | tf_op args[4]
  5.9 184.5 %shard_map.109 = bf16[128,512]{1,0:T(8,128)(2,1)} custom-call(bf16[128,512]{1,0:T(8,128)(2,1)} %attn_ref.1, bf16[512,2048]{1,0:T(8,128)(2,1)} %proj_ref.1, bf16[128,2048]{1,0:T(8,128)(2,1)} %hidden_ref.1, bf16[1,2048]{1,0:T(2,128)(2,1)} %reshape.9.gain_ref, bf16[2048,64]{1,0:T(8,128)(2,1)} %copy.12.router_ref, s32[128,8]{1,0:T(8,128)} %copy.13.routes_ref, ...), custom_call_target="tpu_custom_call" | custom-call | tf_op jit(solution)/shard_map/pallas_call | solution.py:443
  190.4 1.6 copy.15

commit v3 on v2

--- a/solution.py
+++ b/solution.py
@@ -25,21 +25,28 @@
 def layer(
     planes,
     peers,
-    attn_ref,
-    proj_ref,
-    hidden_ref,
+    attn_hbm,
+    proj_hbm,
+    hidden_hbm,
     gain_ref,
-    router_ref,
-    routes_ref,
+    router_hbm,
+    routes_hbm,
     gate_hbm,
     up_hbm,
     down_hbm,
     last_gain_ref,
     source_ref,
     out_ref,
+    attn_ref,
+    proj_ref,
+    hidden_ref,
+    router_ref,
+    routes_ref,
     part,
-    att_send,
-    att_recv,
+    far_send,
+    far_recv,
+    near_send,
+    near_recv,
     res,
     normed,
     gates,
@@ -63,6 +70,7 @@
     pack_recv,
     high,
     low,
+    in_sem,
     own_sem,
     att_s,
     att_r,
@@ -87,7 +95,7 @@
 ):
     x = lax.axis_index("tensor")
     me = lax.axis_index("expert")
-    rows, share = attn_ref.shape
+    rows, share = attn_hbm.shape
     width = planes * share
     slots = slot_send.shape[1]
     all_slots = peers * slots
@@ -108,78 +116,134 @@
     def peer_at(step):
         return lax.rem(me + step, peers)
 
+    barrier = pltpu.get_barrier_semaphore()
+    for d in range(1, planes):
+        pl.semaphore_signal(barrier, inc=1, device_id={"tensor": lax.rem(x + d, planes)})
+
+    @pl.loop(1, peers)
+    def _(step):
+        pl.semaphore_signal(barrier, inc=1, device_id={"expert": peer_at(step)})
+
+    inputs = [
+        pltpu.make_async_copy(src, dst, in_sem.at[i])
+        for i, (src, dst) in enumerate(
+            [
+                (attn_hbm, attn_ref),
+                (proj_hbm, proj_ref),
+                (hidden_hbm, hidden_ref),
+                (router_hbm, router_ref),
+                (routes_hbm, routes_ref),
+            ]
+        )
+    ]
+    for copy in inputs:
+        copy.start()
+
+    piece = share // planes
     own = [
         pltpu.make_async_copy(gate_hbm.at[0], gates.at[0], own_sem.at[0]),
         pltpu.make_async_copy(up_hbm.at[0], ups.at[0], own_sem.at[1]),
     ]
     for j in range(planes):
-        own.append(
-            pltpu.make_async_copy(
-                down_hbm.at[0, :, pl.ds(j * share, share)], downs.at[0, j], own_sem.at[2 + j]
+        for p in range(planes):
+            own.append(
+                pltpu.make_async_copy(
+                    down_hbm.at[0, :, pl.ds(p * share + j * piece, piece)],
+                    downs.at[0, j, :, pl.ds(p * piece, piece)],
+                    own_sem.at[2 + j * planes + p],
+                )
             )
-        )
     for copy in own:
         copy.start()
 
-    barrier = pltpu.get_barrier_semaphore()
-    for d in range(1, planes):
-        pl.semaphore_signal(barrier, inc=1, device_id={"tensor": lax.rem(x + d, planes)})
-
-    @pl.loop(1, peers)
-    def _(step):
-        pl.semaphore_signal(barrier, inc=1, device_id={"expert": peer_at(step)})
-
     ask_send[...] = jnp.broadcast_to(source_ref[...], ask_send.shape)
+    inputs[0].wait()
+    inputs[1].wait()
     for j in range(planes):
         part[j] = dot(attn_ref[...], proj_ref[:, j * share : (j + 1) * share])
-    for d in range(1, planes):
-        att_send[d - 1] = part[lax.rem(x + d, planes)].astype(BF)
+    top, bottom = pl.ds(0, rows // 2), pl.ds(rows // 2, rows // 2)
+    far_send[...] = part[lax.rem(x + 2, planes)].astype(BF)
 
     pl.semaphore_wait(barrier, planes - 1 + peers - 1)
 
-    att = [
-        to_plane(
-            att_send.at[d - 1],
-            att_recv.at[d - 1],
-            att_s.at[d - 1],
-            att_r.at[d - 1],
-            lax.rem(x + d, planes),
-        )
-        for d in range(1, planes)
+    far = [
+        to_plane(far_send.at[top], far_recv.at[0], att_s.at[0], att_r.at[0], right),
+        to_plane(far_send.at[bottom], far_recv.at[1], att_s.at[1], att_r.at[1], left),
     ]
-    for copy in att:
+    for copy in far:
         copy.start()
+
+    fill = width // 8
+
+    def weights_to(hbm, buffer, slot, at, plane):
+        pieces = [
+            to_plane(
+                hbm.at[0, pl.ds(first, count)],
+                buffer.at[slot, pl.ds(first, count)],
+                w_s.at[at],
+                w_r.at[at],
+                plane,
+            )
+            for first, count in ((0, fill), (fill, fill), (2 * fill, fill), (3 * fill, width - 3 * fill))
+        ]
+        return pieces, to_plane(hbm.at[0], buffer.at[slot], w_s.at[at], w_r.at[at], plane)
+
+    gate_r_pieces, gate_r = weights_to(gate_hbm, gates, 1, 0, right)
+    up_r_pieces, up_r = weights_to(up_hbm, ups, 1, 1, right)
+    up_l_pieces, up_l = weights_to(up_hbm, ups, 2, 2, left)
+    gate_l_pieces, gate_l = weights_to(gate_hbm, gates, 2, 3, left)
+    gate_on = to_plane(gates.at[1], gates.at[3], w_s.at[4], w_r.at[4], right)
+    up_on = to_plane(ups.at[2], ups.at[3], w_s.at[5], w_r.at[5], left)
+    gate_r_pieces[0].start()
+    up_l_pieces[0].start()
 
     @pl.loop(1, peers)
     def _(step):
         to_peer(ask_send, ask_recv.at[me], ask_s, ask_r, peer_at(step)).start()
 
-    for copy in att:
+    for copy in far:
+        copy.wait_recv()
+    near_send[0] = part[right].astype(BF)
+    near_send[1] = part[left].astype(BF)
+    near_send[0, top] = (part[right, top] + far_recv[0].astype(F32)).astype(BF)
+    near_send[1, bottom] = (part[left, bottom] + far_recv[1].astype(F32)).astype(BF)
+    near = [
+        to_plane(near_send.at[0], near_recv.at[0], att_s.at[2], att_r.at[2], right),
+        to_plane(near_send.at[1], near_recv.at[1], att_s.at[3], att_r.at[3], left),
+    ]
+    for copy in near:
+        copy.start()
+    gate_r_pieces[1].start()
+    up_l_pieces[1].start()
+    inputs[2].wait()
+    inputs[3].wait()
+    inputs[4].wait()
+    for copy in near:
         copy.wait_recv()
     mine = pl.ds(pl.multiple_of(x * share, share), share)
-    attention = part[x]
-    for d in range(planes - 1):
-        attention = attention + att_recv[d].astype(F32)
+    attention = part[x] + near_recv[0].astype(F32) + near_recv[1].astype(F32)
     res[x] = (hidden_ref[:, mine].astype(F32) + attention).astype(BF)
     spread_res = [
-        to_plane(res.at[x], res.at[x], res_s.at[d - 1], res_r.at[d - 1], lax.rem(x + d, planes))
-        for d in range(1, planes)
+        to_plane(res.at[x], res.at[x], res_s.at[0], res_r.at[0], right),
+        to_plane(res.at[x], res.at[x], res_s.at[1], res_r.at[1], left),
     ]
     for copy in spread_res:
         copy.start()
-
-    gate_r = to_plane(gate_hbm.at[0], gates.at[1], w_s.at[0], w_r.at[0], right)
-    up_r = to_plane(up_hbm.at[0], ups.at[1], w_s.at[1], w_r.at[1], right)
-    up_l = to_plane(up_hbm.at[0], ups.at[2], w_s.at[2], w_r.at[2], left)
-    gate_l = to_plane(gate_hbm.at[0], gates.at[2], w_s.at[3], w_r.at[3], left)
-    gate_on = to_plane(gates.at[1], gates.at[3], w_s.at[4], w_r.at[4], right)
-    up_on = to_plane(ups.at[2], ups.at[3], w_s.at[5], w_r.at[5], left)
-    gate_r.start()
-    up_l.start()
-    up_r.start()
-    gate_l.start()
-
-    for copy in spread_res:
+    gate_r_pieces[2].start()
+    up_l_pieces[2].start()
+    res_on = [
+        to_plane(res.at[left, top], res.at[left, top], res_s.at[2], res_r.at[2], right),
+        to_plane(res.at[right, bottom], res.at[right, bottom], res_s.at[3], res_r.at[3], left),
+    ]
+    for copy, onward in zip(spread_res, res_on):
+        copy.wait_recv()
+        onward.start()
+    gate_r_pieces[3].start()
+    up_l_pieces[3].start()
+    for copy in up_r_pieces + gate_l_pieces:
+        copy.start()
+
+    for copy in res_on:
         copy.wait_recv()
     square = jnp.zeros((rows, 1), F32)
     for j in range(planes):
@@ -190,13 +254,16 @@
     logits = jnp.zeros((rows, experts), F32)
     for j in range(planes):
         cols = slice(j * share, (j + 1) * share)
-        scaled = (res[j].astype(F32) * inverse * gain_ref[:, cols].astype(F32)).astype(BF)
+        scaled = (res[j].astype(F32) * inverse * gain_ref[cols].astype(F32).reshape(1, share)).astype(BF)
         normed[j] = scaled
-        logits = logits + dot(scaled, router_ref[cols, :])
+        logits = logits + lax.dot_general(
+            scaled, router_ref[:, cols], (((1,), (1,)), ((), ())), preferred_element_type=F32
+        )
     named = jnp.zeros((rows, experts), jnp.bool_)
     which = iota((rows, experts), 1)
-    for k in range(routes_ref.shape[1]):
-        named = named | (routes_ref[:, k : k + 1] == which)
+    routed = jnp.transpose(routes_ref[...].astype(F32)).astype(jnp.int32)
+    for k in range(routed.shape[1]):
+        named = named | (routed[:, k : k + 1] == which)
     named_f = jnp.where(named, 1.0, 0.0).astype(F32)
     powers = jnp.where(named, jnp.exp(logits), 0.0)
     weights = powers / jnp.sum(powers, axis=1, keepdims=True)
@@ -223,7 +290,7 @@
         peer = peer_at(step)
         to_peer(slot_send.at[peer], slot_recv.at[me], slot_s, slot_r, peer).start()
 
-    own_slot = pltpu.make_async_copy(slot_send.at[me], slot_recv.at[me], own_sem.at[2 + planes])
+    own_slot = pltpu.make_async_copy(slot_send.at[me], slot_recv.at[me], own_sem.at[2 + planes * planes])
     own_slot.start()
 
     gate_r.wait_recv()
@@ -234,27 +301,33 @@
     half = hidden_units // 2
     down_r, down_l, on_r, on_l = [], [], [], []
     for j in range(planes):
-        cols = pl.ds(j * share, share)
-        down_r.append(
-            to_plane(down_hbm.at[0, :, cols], downs.at[1, j], d_s.at[0, j], d_r.at[0, j], right)
-        )
-        down_l.append(
-            to_plane(down_hbm.at[0, :, cols], downs.at[2, j], d_s.at[1, j], d_r.at[1, j], left)
-        )
-        top, bottom = pl.ds(0, half), pl.ds(half, half)
+        down_r.append(to_plane(downs.at[0, j], downs.at[1, j], d_s.at[0, j], d_r.at[0, j], right))
+        down_l.append(to_plane(downs.at[0, j], downs.at[2, j], d_s.at[1, j], d_r.at[1, j], left))
+        upper, lower = pl.ds(0, half), pl.ds(half, half)
         on_r.append(
             to_plane(
-                downs.at[1, j, top], downs.at[3, j, top], d_s.at[2, j], d_r.at[2, j], right
+                downs.at[1, j, upper], downs.at[3, j, upper], d_s.at[2, j], d_r.at[2, j], right
             )
         )
         on_l.append(
             to_plane(
-                downs.at[2, j, bottom], downs.at[3, j, bottom], d_s.at[3, j], d_r.at[3, j], left
+                downs.at[2, j, lower], downs.at[3, j, lower], d_s.at[3, j], d_r.at[3, j], left
             )
         )
+    for copy in own[2:]:
+        copy.wait()
     for j in range(2):
         down_r[j].start()
         down_l[j].start()
+
+    def pass_down(j):
+        down_r[j].wait_recv()
+        on_r[j].start()
+        down_l[j].wait_recv()
+        on_l[j].start()
+        if j + 2 < planes:
+            down_r[j + 2].start()
+            down_l[j + 2].start()
 
     everyone = pl.ds(0, peers - 1)
     to_peer(slot_send.at[everyone], slot_recv.at[everyone], slot_s, slot_r, me).wait_recv()
@@ -280,16 +353,7 @@
     gate_l.wait_recv()
     activate(2)
 
-    for copy in own[2:]:
-        copy.wait()
-    down_r[0].wait_recv()
-    on_r[0].start()
-    down_l[0].wait_recv()
-    on_l[0].start()
-    for j in range(2, planes):
-        down_r[j].start()
-        down_l[j].start()
-
+    pass_down(0)
     gate_on.wait_recv()
     up_on.wait_recv()
     activate(3)
@@ -300,22 +364,15 @@
         ).wait_recv()
         back = back_recv[j].reshape(all_slots, share)
         mixed = dot(high[...], back) + dot(low[...], back)
-        mix_send[j] = mixed.astype(BF)
-
-        @pl.when(x == j)
-        def _():
-            mix_own[...] = mixed
-
-        @pl.when(x != j)
-        def _():
-            to_plane(mix_send.at[j], mix_recv.at[x], mix_s, mix_r, j).start()
-
-    for j in range(planes):
-        if j + 1 < planes:
-            down_r[j + 1].wait_recv()
-            on_r[j + 1].start()
-            down_l[j + 1].wait_recv()
-            on_l[j + 1].start()
+        for p in range(planes):
+            mix_send[j, p] = mixed[:, p * piece : (p + 1) * piece].astype(BF)
+            mix_own[p] = mixed[:, p * piece : (p + 1) * piece]
+        total[:, j * piece : (j + 1) * piece] = mix_own[x]
+        for d in range(1, planes):
+            plane = lax.rem(x + d, planes)
+            to_plane(mix_send.at[j, plane], mix_recv.at[d - 1, j], mix_s, mix_r, plane).start()
+
+    def produce(j):
         on_r[j].wait_recv()
         on_l[j].wait_recv()
         product = dot(acts[0], downs[0, j])
@@ -331,20 +388,30 @@
                 back_send.at[j, peer], back_recv.at[j, me], back_s.at[j], back_r.at[j], peer
             ).start()
 
-        if j >= 1:
-            combine(j - 1)
-    combine(planes - 1)
+    pass_down(1)
+    produce(0)
+    pass_down(2)
+    produce(1)
+    pass_down(3)
+    produce(2)
+    combine(0)
+    produce(3)
+    combine(1)
+    combine(2)
+    combine(3)
 
     three = pl.ds(0, planes - 1)
-    to_plane(mix_send.at[three], mix_recv.at[three], mix_s, mix_r, x).wait_recv()
-    whole = mix_own[...] + res[x].astype(F32)
-    for j in range(planes):
-        whole = whole + jnp.where(x == j, 0.0, mix_recv[j].astype(F32))
+    to_plane(mix_recv.at[three], mix_recv.at[three], mix_s, mix_r, x).wait_recv()
+    mixture = [total[:, j * piece : (j + 1) * piece] for j in range(planes)]
+    for j in range(planes):
+        for d in range(planes - 1):
+            mixture[j] = mixture[j] + mix_recv[d, j].astype(F32)
+    whole = jnp.concatenate(mixture, axis=1) + res[x].astype(F32)
     total[...] = whole
     squares = jnp.zeros((rows, 128), F32)
     for c in range(share // 128):
-        piece = whole[:, c * 128 : (c + 1) * 128]
-        squares = squares + piece * piece
+        part_of = whole[:, c * 128 : (c + 1) * 128]
+        squares = squares + part_of * part_of
     row_sum = jnp.sum(jnp.transpose(squares), axis=0, keepdims=True)
     sq_send[...] = jnp.broadcast_to(row_sum, sq_send.shape)
     sq = [
@@ -373,7 +440,7 @@
         sums = sums + sq_recv[d]
     column = jnp.transpose(jnp.broadcast_to(sums[0:1], (rows, rows)))[:, 0:1]
     scale = lax.rsqrt(column / width + epsilon)
-    result = (total[...] * scale * last_gain_ref[...].astype(F32)).astype(BF)
+    result = (total[...] * scale * last_gain_ref[...].astype(F32).reshape(1, share)).astype(BF)
     packed = jnp.zeros((peers * 8, 128), F32)
     for c in range(4):
         chooser = jnp.where(wanted & (line % 4 == c), 1.0, 0.0).astype(BF)
@@ -399,7 +466,7 @@
         out_ref[:, c * 128 : (c + 1) * 128] = dot(chooser, landed).astype(BF)
 
     for copy in (
-        att + spread_res + [gate_r, up_r, up_l, gate_l, gate_on, up_on]
+        far + near + spread_res + res_on + [gate_r, up_r, up_l, gate_l, gate_on, up_on]
         + down_r + down_l + on_r + on_l + sq
     ):
         copy.wait_send()
@@ -413,7 +480,7 @@
         to_peer(
             back_send.at[j, everyone], back_recv.at[j, everyone], back_s.at[j], back_r.at[j], me
         ).wait_send()
-    to_plane(mix_send.at[three], mix_recv.at[three], mix_s, mix_r, x).wait_send()
+    to_plane(mix_send.at[:, three], mix_recv.at[three], mix_s, mix_r, x).wait_send()
     to_peer(pack_send.at[everyone], pack_recv.at[everyone], pack_s, pack_r, me).wait_send()
 
 
@@ -443,12 +510,19 @@
         return pl.pallas_call(
             functools.partial(layer, planes, peers),
             out_shape=jax.ShapeDtypeStruct((rows, share), BF),
-            in_specs=[local] * 6 + [remote] * 3 + [local] * 2,
+            in_specs=[remote] * 3 + [local] + [remote] * 5 + [local] * 2,
             out_specs=local,
             scratch_shapes=[
+                VMEM((rows, share), BF),
+                VMEM((share, width), BF),
+                VMEM((rows, width), BF),
+                VMEM((peers, width), BF),
+                VMEM((top, rows), jnp.int32),
                 VMEM((planes, rows, share), F32),
-                VMEM((planes - 1, rows, share), BF),
-                VMEM((planes - 1, rows, share), BF),
+                VMEM((rows, share), BF),
+                VMEM((2, rows // 2, share), BF),
+                VMEM((2, rows, share), BF),
+                VMEM((2, rows, share), BF),
                 VMEM((planes, rows, share), BF),
                 VMEM((planes, rows, share), BF),
                 VMEM((planes, width, units), BF),
@@ -462,9 +536,9 @@
                 VMEM((planes, peers * slots, units), BF),
                 VMEM((planes, peers, slots, share), BF),
                 VMEM((planes, peers, slots, share), BF),
-                VMEM((planes, rows, share), BF),
-                VMEM((planes, rows, share), BF),
-                VMEM((rows, share), F32),
+                VMEM((planes, planes, rows, share // planes), BF),
+                VMEM((planes - 1, planes, rows, share // planes), BF),
+                VMEM((planes, rows, share // planes), F32),
                 VMEM((rows, share), F32),
                 VMEM((8, rows), F32),
                 VMEM((planes - 1, 8, rows), F32),
@@ -472,11 +546,12 @@
                 VMEM((peers, 8, 128), BF),
                 VMEM((rows, peers * slots), BF),
                 VMEM((rows, peers * slots), BF),
-                DMA((3 + planes,)),
-                DMA((planes - 1,)),
-                DMA((planes - 1,)),
-                DMA((planes - 1,)),
-                DMA((planes - 1,)),
+                DMA((5,)),
+                DMA((3 + planes * planes,)),
+                DMA((4,)),
+                DMA((4,)),
+                DMA((4,)),
+                DMA((4,)),
                 DMA,
                 DMA,
                 DMA,
@@ -501,13 +576,13 @@
             attn_out,
             out_proj,
             hidden_in,
-            norm_gain.reshape(1, width),
-            router,
-            routes,
+            norm_gain,
+            router.T,
+            routes.T,
             w_gate,
             w_up,
             w_down,
-            final_gain.reshape(1, share),
+            final_gain,
             source.reshape(1, rows),
         )
 

time: 192 us -> 174 us (0.906)
  Pallas kernels: 185 us -> 172 us
  local copies, waits for them, and re-layouts: 7.46 us -> 1.57 us
    pallas_call x1, Pallas kernels: 185 us -> 172 us  [on_device(): pl.pallas_call(functools.partial(layer, planes, peers), out_shape=jax.Sha...]
    unnamed x3 -> x1, local copies, waits for them, and re-layouts: 4.93 us -> 1.57 us
    reshape x2 -> x0, local copies, waits for them, and re-layouts: 2.53 us -> none  [the longest x1 1.27 us: on_device(): norm_gain.reshape(1, width)]
where the time goes in v3:
time: 174 us
  Pallas kernels  172 us (99%)
    pallas_call x1, Pallas kernels, on_device(): pl.pallas_call(functools.partial(layer, planes, peers), out_shape=jax.Sha...  172 us

profile of v3, /device:TPU:1, one launch (start us, length us, event | category | flops | bytes accessed | tf_op | source)
XLA Modules:
  0.0 173.7 jit_solution(1518212545962489679)
XLA Ops:
  0.0 172.1 %shard_map.109 = bf16[128,512]{1,0:T(8,128)(2,1)} custom-call(bf16[128,512]{1,0:T(8,128)(2,1)} %attn_hbm.1, bf16[512,2048]{1,0:T(8,128)(2,1)} %proj_hbm.1, bf16[128,2048]{1,0:T(8,128)(2,1)} %hidden_hbm.1, bf16[2048]{0:T(1024)(128)(2,1)} %gain_ref.1, bf16[64,2048]{1,0:T(8,128)(2,1)} %bitcast.3, s32[8,128]{1,0:T(8,128)} %bitcast.4, ...), custom_call_target="tpu_custom_call" | custom-call | tf_op jit(solution)/shard_map/pallas_call | solution.py:510
  172.1 1.6 copy.13

commit v4 on v3

--- a/solution.py
+++ b/solution.py
@@ -28,20 +28,23 @@
     attn_hbm,
     proj_hbm,
     hidden_hbm,
-    gain_ref,
+    gain_hbm,
     router_hbm,
     routes_hbm,
     gate_hbm,
     up_hbm,
     down_hbm,
-    last_gain_ref,
-    source_ref,
+    last_gain_hbm,
+    source_hbm,
     out_ref,
     attn_ref,
     proj_ref,
     hidden_ref,
     router_ref,
     routes_ref,
+    gain_ref,
+    last_gain_ref,
+    source_ref,
     part,
     far_send,
     far_recv,
@@ -62,7 +65,6 @@
     back_recv,
     mix_send,
     mix_recv,
-    mix_own,
     total,
     sq_send,
     sq_recv,
@@ -133,6 +135,9 @@
                 (hidden_hbm, hidden_ref),
                 (router_hbm, router_ref),
                 (routes_hbm, routes_ref),
+                (gain_hbm, gain_ref),
+                (last_gain_hbm, last_gain_ref),
+                (source_hbm, source_ref),
             ]
         )
     ]
@@ -140,22 +145,25 @@
         copy.start()
 
     piece = share // planes
+    chunks = 2 * planes
     own = [
         pltpu.make_async_copy(gate_hbm.at[0], gates.at[0], own_sem.at[0]),
         pltpu.make_async_copy(up_hbm.at[0], ups.at[0], own_sem.at[1]),
     ]
-    for j in range(planes):
-        for p in range(planes):
+    for c in range(chunks):
+        for i in range(2):
+            first = (c % 2 * 2 + i) * share + c // 2 * piece
             own.append(
                 pltpu.make_async_copy(
-                    down_hbm.at[0, :, pl.ds(p * share + j * piece, piece)],
-                    downs.at[0, j, :, pl.ds(p * piece, piece)],
-                    own_sem.at[2 + j * planes + p],
+                    down_hbm.at[0, :, pl.ds(first, piece)],
+                    downs.at[0, c, :, pl.ds(i * piece, piece)],
+                    own_sem.at[2 + 2 * c + i],
                 )
             )
     for copy in own:
         copy.start()
 
+    inputs[7].wait()
     ask_send[...] = jnp.broadcast_to(source_ref[...], ask_send.shape)
     inputs[0].wait()
     inputs[1].wait()
@@ -215,9 +223,8 @@
         copy.start()
     gate_r_pieces[1].start()
     up_l_pieces[1].start()
-    inputs[2].wait()
-    inputs[3].wait()
-    inputs[4].wait()
+    for copy in inputs[2:7]:
+        copy.wait()
     for copy in near:
         copy.wait_recv()
     mine = pl.ds(pl.multiple_of(x * share, share), share)
@@ -254,7 +261,8 @@
     logits = jnp.zeros((rows, experts), F32)
     for j in range(planes):
         cols = slice(j * share, (j + 1) * share)
-        scaled = (res[j].astype(F32) * inverse * gain_ref[cols].astype(F32).reshape(1, share)).astype(BF)
+        gain = gain_ref[cols].astype(F32).reshape(1, share)
+        scaled = (res[j].astype(F32) * inverse * gain).astype(BF)
         normed[j] = scaled
         logits = logits + lax.dot_general(
             scaled, router_ref[:, cols], (((1,), (1,)), ((), ())), preferred_element_type=F32
@@ -290,44 +298,46 @@
         peer = peer_at(step)
         to_peer(slot_send.at[peer], slot_recv.at[me], slot_s, slot_r, peer).start()
 
-    own_slot = pltpu.make_async_copy(slot_send.at[me], slot_recv.at[me], own_sem.at[2 + planes * planes])
+    own_slot = pltpu.make_async_copy(slot_send.at[me], slot_recv.at[me], own_sem.at[2 + 2 * chunks])
     own_slot.start()
 
+    half = hidden_units // 2
+    upper, lower = pl.ds(0, half), pl.ds(half, half)
+    down_r, down_l, on_r, on_l = [], [], [], []
+    for c in range(chunks):
+        down_r.append(to_plane(downs.at[0, c], downs.at[1, c], d_s.at[0, c], d_r.at[0, c], right))
+        down_l.append(to_plane(downs.at[0, c], downs.at[2, c], d_s.at[1, c], d_r.at[1, c], left))
+        on_r.append(
+            to_plane(
+                downs.at[1, c, upper], downs.at[3, c, upper], d_s.at[2, c], d_r.at[2, c], right
+            )
+        )
+        on_l.append(
+            to_plane(
+                downs.at[2, c, lower], downs.at[3, c, lower], d_s.at[3, c], d_r.at[3, c], left
+            )
+        )
+
+    def send_down(c):
+        down_r[c].start()
+        down_l[c].start()
+
+    def pass_down(c):
+        down_r[c].wait_recv()
+        on_r[c].start()
+        down_l[c].wait_recv()
+        on_l[c].start()
+
+    for copy in own[2:]:
+        copy.wait()
+    send_down(0)
     gate_r.wait_recv()
     gate_on.start()
     up_l.wait_recv()
     up_on.start()
-
-    half = hidden_units // 2
-    down_r, down_l, on_r, on_l = [], [], [], []
-    for j in range(planes):
-        down_r.append(to_plane(downs.at[0, j], downs.at[1, j], d_s.at[0, j], d_r.at[0, j], right))
-        down_l.append(to_plane(downs.at[0, j], downs.at[2, j], d_s.at[1, j], d_r.at[1, j], left))
-        upper, lower = pl.ds(0, half), pl.ds(half, half)
-        on_r.append(
-            to_plane(
-                downs.at[1, j, upper], downs.at[3, j, upper], d_s.at[2, j], d_r.at[2, j], right
-            )
-        )
-        on_l.append(
-            to_plane(
-                downs.at[2, j, lower], downs.at[3, j, lower], d_s.at[3, j], d_r.at[3, j], left
-            )
-        )
-    for copy in own[2:]:
-        copy.wait()
-    for j in range(2):
-        down_r[j].start()
-        down_l[j].start()
-
-    def pass_down(j):
-        down_r[j].wait_recv()
-        on_r[j].start()
-        down_l[j].wait_recv()
-        on_l[j].start()
-        if j + 2 < planes:
-            down_r[j + 2].start()
-            down_l[j + 2].start()
+    pass_down(0)
+    send_down(1)
+    send_down(2)
 
     everyone = pl.ds(0, peers - 1)
     to_peer(slot_send.at[everyone], slot_recv.at[everyone], slot_s, slot_r, me).wait_recv()
@@ -353,7 +363,6 @@
     gate_l.wait_recv()
     activate(2)
 
-    pass_down(0)
     gate_on.wait_recv()
     up_on.wait_recv()
     activate(3)
@@ -362,15 +371,24 @@
         to_peer(
             back_send.at[j, everyone], back_recv.at[j, everyone], back_s.at[j], back_r.at[j], me
         ).wait_recv()
-        back = back_recv[j].reshape(all_slots, share)
+        back = back_recv[j].reshape(all_slots, 2 * piece)
         mixed = dot(high[...], back) + dot(low[...], back)
-        for p in range(planes):
-            mix_send[j, p] = mixed[:, p * piece : (p + 1) * piece].astype(BF)
-            mix_own[p] = mixed[:, p * piece : (p + 1) * piece]
-        total[:, j * piece : (j + 1) * piece] = mix_own[x]
-        for d in range(1, planes):
-            plane = lax.rem(x + d, planes)
-            to_plane(mix_send.at[j, plane], mix_recv.at[d - 1, j], mix_s, mix_r, plane).start()
+        at = j // 2
+        for i in range(2):
+            plane = j % 2 * 2 + i
+            part_of = mixed[:, i * piece : (i + 1) * piece]
+            mix_send[at, plane] = part_of.astype(BF)
+
+            @pl.when(x == plane)
+            def _():
+                total[:, at * piece : (at + 1) * piece] = part_of
+
+            @pl.when(x != plane)
+            def _():
+                slot = lax.rem(x - plane + planes, planes) - 1
+                to_plane(
+                    mix_send.at[at, plane], mix_recv.at[slot, at], mix_s, mix_r, plane
+                ).start()
 
     def produce(j):
         on_r[j].wait_recv()
@@ -378,7 +396,7 @@
         product = dot(acts[0], downs[0, j])
         for q in range(1, planes):
             product = product + dot(acts[q], downs[q, j])
-        back_send[j] = product.astype(BF).reshape(peers, slots, share)
+        back_send[j] = product.astype(BF).reshape(peers, slots, 2 * piece)
         back_recv[j, me] = back_send[j, me]
 
         @pl.loop(1, peers)
@@ -388,17 +406,18 @@
                 back_send.at[j, peer], back_recv.at[j, me], back_s.at[j], back_r.at[j], peer
             ).start()
 
-    pass_down(1)
     produce(0)
-    pass_down(2)
-    produce(1)
-    pass_down(3)
-    produce(2)
-    combine(0)
-    produce(3)
-    combine(1)
-    combine(2)
-    combine(3)
+    for c in range(1, chunks):
+        pass_down(c)
+        if c + 2 < chunks:
+            send_down(c + 2)
+        if c >= 2:
+            produce(c - 1)
+        if c == 5:
+            combine(0)
+    produce(chunks - 1)
+    for c in range(1, chunks):
+        combine(c)
 
     three = pl.ds(0, planes - 1)
     to_plane(mix_recv.at[three], mix_recv.at[three], mix_s, mix_r, x).wait_recv()
@@ -440,7 +459,8 @@
         sums = sums + sq_recv[d]
     column = jnp.transpose(jnp.broadcast_to(sums[0:1], (rows, rows)))[:, 0:1]
     scale = lax.rsqrt(column / width + epsilon)
-    result = (total[...] * scale * last_gain_ref[...].astype(F32).reshape(1, share)).astype(BF)
+    last_gain = last_gain_ref[...].astype(F32).reshape(1, share)
+    result = (total[...] * scale * last_gain).astype(BF)
     packed = jnp.zeros((peers * 8, 128), F32)
     for c in range(4):
         chooser = jnp.where(wanted & (line % 4 == c), 1.0, 0.0).astype(BF)
@@ -459,28 +479,28 @@
     later = jnp.max(jnp.where(same, 1, 0), axis=1, keepdims=True)
     place = (asks_down[:, 0:1] // rows) * 8 + later * 4
     at = iota((rows, peers * 8), 1)
+    for copy in (
+        far + near + spread_res + res_on + [gate_r, up_r, up_l, gate_l, gate_on, up_on]
+        + down_r + down_l + on_r + on_l + sq
+    ):
+        copy.wait_send()
+
+    @pl.loop(1, peers)
+    def _(step):
+        to_peer(ask_send, ask_recv.at[me], ask_s, ask_r, me).wait_send()
+
+    to_peer(slot_send.at[everyone], slot_recv.at[everyone], slot_s, slot_r, me).wait_send()
+    for j in range(chunks):
+        to_peer(
+            back_send.at[j, everyone], back_recv.at[j, everyone], back_s.at[j], back_r.at[j], me
+        ).wait_send()
+    to_plane(mix_send.at[:, three], mix_recv.at[three], mix_s, mix_r, x).wait_send()
     to_peer(pack_send.at[everyone], pack_recv.at[everyone], pack_s, pack_r, me).wait_recv()
     landed = pack_recv[...].reshape(peers * 8, 128)
     for c in range(4):
         chooser = jnp.where(at == place + c, 1.0, 0.0).astype(BF)
         out_ref[:, c * 128 : (c + 1) * 128] = dot(chooser, landed).astype(BF)
 
-    for copy in (
-        far + near + spread_res + res_on + [gate_r, up_r, up_l, gate_l, gate_on, up_on]
-        + down_r + down_l + on_r + on_l + sq
-    ):
-        copy.wait_send()
-
-    @pl.loop(1, peers)
-    def _(step):
-        to_peer(ask_send, ask_recv.at[me], ask_s, ask_r, me).wait_send()
-
-    to_peer(slot_send.at[everyone], slot_recv.at[everyone], slot_s, slot_r, me).wait_send()
-    for j in range(planes):
-        to_peer(
-            back_send.at[j, everyone], back_recv.at[j, everyone], back_s.at[j], back_r.at[j], me
-        ).wait_send()
-    to_plane(mix_send.at[:, three], mix_recv.at[three], mix_s, mix_r, x).wait_send()
     to_peer(pack_send.at[everyone], pack_recv.at[everyone], pack_s, pack_r, me).wait_send()
 
 
@@ -510,7 +530,7 @@
         return pl.pallas_call(
             functools.partial(layer, planes, peers),
             out_shape=jax.ShapeDtypeStruct((rows, share), BF),
-            in_specs=[remote] * 3 + [local] + [remote] * 5 + [local] * 2,
+            in_specs=[remote] * 11,
             out_specs=local,
             scratch_shapes=[
                 VMEM((rows, share), BF),
@@ -518,6 +538,9 @@
                 VMEM((rows, width), BF),
                 VMEM((peers, width), BF),
                 VMEM((top, rows), jnp.int32),
+                VMEM((width,), BF),
+                VMEM((share,), BF),
+                VMEM((1, rows), jnp.int32),
                 VMEM((planes, rows, share), F32),
                 VMEM((rows, share), BF),
                 VMEM((2, rows // 2, share), BF),
@@ -527,18 +550,17 @@
                 VMEM((planes, rows, share), BF),
                 VMEM((planes, width, units), BF),
                 VMEM((planes, width, units), BF),
-                VMEM((planes, planes, units, share), BF),
+                VMEM((planes, 2 * planes, units, share // 2), BF),
                 VMEM((8, rows), jnp.int32),
                 VMEM((peers, 8, rows), jnp.int32),
                 VMEM((peers, slots, width), BF),
                 VMEM((peers, slots, width), BF),
                 VMEM((peers * slots, width), BF),
                 VMEM((planes, peers * slots, units), BF),
-                VMEM((planes, peers, slots, share), BF),
-                VMEM((planes, peers, slots, share), BF),
+                VMEM((2 * planes, peers, slots, share // 2), BF),
+                VMEM((2 * planes, peers, slots, share // 2), BF),
                 VMEM((planes, planes, rows, share // planes), BF),
                 VMEM((planes - 1, planes, rows, share // planes), BF),
-                VMEM((planes, rows, share // planes), F32),
                 VMEM((rows, share), F32),
                 VMEM((8, rows), F32),
                 VMEM((planes - 1, 8, rows), F32),
@@ -546,8 +568,8 @@
                 VMEM((peers, 8, 128), BF),
                 VMEM((rows, peers * slots), BF),
                 VMEM((rows, peers * slots), BF),
-                DMA((5,)),
-                DMA((3 + planes * planes,)),
+                DMA((8,)),
+                DMA((3 + 4 * planes,)),
                 DMA((4,)),
                 DMA((4,)),
                 DMA((4,)),
@@ -558,10 +580,10 @@
                 DMA,
                 DMA((6,)),
                 DMA((6,)),
-                DMA((4, planes)),
-                DMA((4, planes)),
-                DMA((planes,)),
-                DMA((planes,)),
+                DMA((4, 2 * planes)),
+                DMA((4, 2 * planes)),
+                DMA((2 * planes,)),
+                DMA((2 * planes,)),
                 DMA,
                 DMA,
                 DMA((planes - 1,)),

time: 174 us -> 165 us (0.948)
  Pallas kernels: 172 us -> 163 us
    pallas_call x1, Pallas kernels: 172 us -> 163 us  [on_device(): pl.pallas_call(functools.partial(layer, planes, peers), out_shape=jax.Sha...]
where the time goes in v4:
time: 165 us
  Pallas kernels  163 us (99%)
    pallas_call x1, Pallas kernels, on_device(): pl.pallas_call(functools.partial(layer, planes, peers), out_shape=jax.Sha...  163 us

profile of v4, /device:TPU:1, one launch (start us, length us, event | category | flops | bytes accessed | tf_op | source)
XLA Modules:
  0.0 165.0 jit_solution(15550094669859784296)
XLA Ops:
  0.0 163.4 %shard_map.109 = bf16[128,512]{1,0:T(8,128)(2,1)} custom-call(bf16[128,512]{1,0:T(8,128)(2,1)} %attn_hbm.1, bf16[512,2048]{1,0:T(8,128)(2,1)} %proj_hbm.1, bf16[128,2048]{1,0:T(8,128)(2,1)} %hidden_hbm.1, bf16[2048]{0:T(1024)(128)(2,1)} %gain_hbm.1, bf16[64,2048]{1,0:T(8,128)(2,1)} %bitcast.3, s32[8,128]{1,0:T(8,128)} %bitcast.4, ...), custom_call_target="tpu_custom_call" | custom-call | tf_op jit(solution)/shard_map/pallas_call | solution.py:530
  163.4 1.6 copy.13

commit v5 on v4

--- a/solution.py
+++ b/solution.py
@@ -55,6 +55,7 @@
     gates,
     ups,
     downs,
+    stage,
     ask_send,
     ask_recv,
     slot_send,
@@ -104,12 +105,27 @@
     hidden_units = gate_hbm.shape[2]
     right = lax.rem(x + 1, planes)
     left = lax.rem(x + planes - 1, planes)
+    active = x // 2
+    host = lax.rem(me, 2) == active
+    guest = jnp.logical_not(host)
+    partner = x + 1 - 2 * lax.rem(x, 2)
+    outer = planes - 1 - x
+    sibling = me + 1 - 2 * lax.rem(me, 2)
 
     def to_plane(src, dst, send, recv, plane):
         return pltpu.make_async_remote_copy(
             src_ref=src, dst_ref=dst, send_sem=send, recv_sem=recv, device_id={"tensor": plane}
         )
 
+    def to_device(src, dst, send, recv, plane, peer):
+        return pltpu.make_async_remote_copy(
+            src_ref=src,
+            dst_ref=dst,
+            send_sem=send,
+            recv_sem=recv,
+            device_id={"tensor": plane, "expert": peer},
+        )
+
     def to_peer(src, dst, send, recv, peer):
         return pltpu.make_async_remote_copy(
             src_ref=src, dst_ref=dst, send_sem=send, recv_sem=recv, device_id={"expert": peer}
@@ -121,6 +137,7 @@
     barrier = pltpu.get_barrier_semaphore()
     for d in range(1, planes):
         pl.semaphore_signal(barrier, inc=1, device_id={"tensor": lax.rem(x + d, planes)})
+    pl.semaphore_signal(barrier, inc=1, device_id={"tensor": outer, "expert": sibling})
 
     @pl.loop(1, peers)
     def _(step):
@@ -150,18 +167,33 @@
         pltpu.make_async_copy(gate_hbm.at[0], gates.at[0], own_sem.at[0]),
         pltpu.make_async_copy(up_hbm.at[0], ups.at[0], own_sem.at[1]),
     ]
-    for c in range(chunks):
+
+    def own_down(c, buffer):
+        copies = []
         for i in range(2):
             first = (c % 2 * 2 + i) * share + c // 2 * piece
-            own.append(
+            copies.append(
                 pltpu.make_async_copy(
                     down_hbm.at[0, :, pl.ds(first, piece)],
-                    downs.at[0, c, :, pl.ds(i * piece, piece)],
+                    buffer.at[c, :, pl.ds(i * piece, piece)],
                     own_sem.at[2 + 2 * c + i],
                 )
             )
-    for copy in own:
-        copy.start()
+        return copies
+
+    @pl.when(host)
+    def _():
+        for copy in own:
+            copy.start()
+        for c in range(chunks):
+            for copy in own_down(c, downs.at[0]):
+                copy.start()
+
+    @pl.when(guest)
+    def _():
+        for c in range(chunks):
+            for copy in own_down(c, stage):
+                copy.start()
 
     inputs[7].wait()
     ask_send[...] = jnp.broadcast_to(source_ref[...], ask_send.shape)
@@ -172,7 +204,7 @@
     top, bottom = pl.ds(0, rows // 2), pl.ds(rows // 2, rows // 2)
     far_send[...] = part[lax.rem(x + 2, planes)].astype(BF)
 
-    pl.semaphore_wait(barrier, planes - 1 + peers - 1)
+    pl.semaphore_wait(barrier, planes - 1 + 1 + peers - 1)
 
     far = [
         to_plane(far_send.at[top], far_recv.at[0], att_s.at[0], att_r.at[0], right),
@@ -181,29 +213,47 @@
     for copy in far:
         copy.start()
 
-    fill = width // 8
-
-    def weights_to(hbm, buffer, slot, at, plane):
-        pieces = [
-            to_plane(
-                hbm.at[0, pl.ds(first, count)],
-                buffer.at[slot, pl.ds(first, count)],
-                w_s.at[at],
-                w_r.at[at],
-                plane,
-            )
-            for first, count in ((0, fill), (fill, fill), (2 * fill, fill), (3 * fill, width - 3 * fill))
-        ]
-        return pieces, to_plane(hbm.at[0], buffer.at[slot], w_s.at[at], w_r.at[at], plane)
-
-    gate_r_pieces, gate_r = weights_to(gate_hbm, gates, 1, 0, right)
-    up_r_pieces, up_r = weights_to(up_hbm, ups, 1, 1, right)
-    up_l_pieces, up_l = weights_to(up_hbm, ups, 2, 2, left)
-    gate_l_pieces, gate_l = weights_to(gate_hbm, gates, 2, 3, left)
-    gate_on = to_plane(gates.at[1], gates.at[3], w_s.at[4], w_r.at[4], right)
-    up_on = to_plane(ups.at[2], ups.at[3], w_s.at[5], w_r.at[5], left)
-    gate_r_pieces[0].start()
-    up_l_pieces[0].start()
+    fill = width // 16
+    middle = width // 2
+    units_of = [(gates, gate_hbm, 0), (gates, gate_hbm, middle), (ups, up_hbm, 0), (ups, up_hbm, middle)]
+
+    def unit_view(slot, u):
+        buffer, _, first = units_of[u]
+        return buffer.at[slot, pl.ds(first, middle)]
+
+    def own_unit(u, slot, kind, plane, peer, first=0, count=middle):
+        buffer, hbm, base = units_of[u]
+        return to_device(
+            hbm.at[0, pl.ds(base + first, count)],
+            buffer.at[slot, pl.ds(base + first, count)],
+            w_s.at[kind, u],
+            w_r.at[slot, u],
+            plane,
+            peer,
+        )
+
+    def onward_unit(u, slot, there, kind, plane, peer):
+        return to_device(
+            unit_view(slot, u), unit_view(there, u), w_s.at[kind, u], w_r.at[there, u], plane, peer
+        )
+
+    def unit_arrived(slot, u):
+        own_unit(u, slot, 0, x, me).wait_recv()
+
+    def send_units(first, count, later):
+        @pl.when(host)
+        def _():
+            own_unit(0, 1, 0, partner, me, first, count).start()
+            for u in range(1, 4 if later else 1):
+                own_unit(u, 1, 0, partner, me).start()
+
+        @pl.when(guest)
+        def _():
+            own_unit(0, 2, 0, outer, sibling, first, count).start()
+            for u in range(1, 4 if later else 1):
+                own_unit(u, 2, 0, outer, sibling).start()
+
+    send_units(0, fill, False)
 
     @pl.loop(1, peers)
     def _(step):
@@ -221,8 +271,7 @@
     ]
     for copy in near:
         copy.start()
-    gate_r_pieces[1].start()
-    up_l_pieces[1].start()
+    send_units(fill, fill, False)
     for copy in inputs[2:7]:
         copy.wait()
     for copy in near:
@@ -236,8 +285,7 @@
     ]
     for copy in spread_res:
         copy.start()
-    gate_r_pieces[2].start()
-    up_l_pieces[2].start()
+    send_units(2 * fill, fill, False)
     res_on = [
         to_plane(res.at[left, top], res.at[left, top], res_s.at[2], res_r.at[2], right),
         to_plane(res.at[right, bottom], res.at[right, bottom], res_s.at[3], res_r.at[3], left),
@@ -245,10 +293,13 @@
     for copy, onward in zip(spread_res, res_on):
         copy.wait_recv()
         onward.start()
-    gate_r_pieces[3].start()
-    up_l_pieces[3].start()
-    for copy in up_r_pieces + gate_l_pieces:
-        copy.start()
+    send_units(3 * fill, middle - 3 * fill, True)
+
+    @pl.when(host)
+    def _():
+        for u in range(4):
+            own_unit(u, 0, 1, x, sibling).start()
+
 
     for copy in res_on:
         copy.wait_recv()
@@ -278,11 +329,13 @@
     before = jnp.where(iota((rows, rows), 1) < iota((rows, rows), 0), 1.0, 0.0).astype(BF)
     rank = dot(before, named_f.astype(BF))
     wide = jnp.where(
-        iota((experts, all_slots), 1) // slots == iota((experts, all_slots), 0), 1.0, 0.0
+        iota((experts, all_slots), 1) // (2 * slots) * 2 + active == iota((experts, all_slots), 0),
+        1.0,
+        0.0,
     ).astype(BF)
     wide_rank = dot(rank.astype(BF), wide)
     wide_named = dot(named_f.astype(BF), wide)
-    turn = (iota((rows, all_slots), 1) % slots + x * slots).astype(F32)
+    turn = (iota((rows, all_slots), 1) % (2 * slots) + lax.rem(x, 2) * 2 * slots).astype(F32)
     taken = (wide_named > 0.5) & (wide_rank == turn)
     weights_high = weights.astype(BF)
     weights_low = (weights - weights_high.astype(F32)).astype(BF)
@@ -301,46 +354,62 @@
     own_slot = pltpu.make_async_copy(slot_send.at[me], slot_recv.at[me], own_sem.at[2 + 2 * chunks])
     own_slot.start()
 
-    half = hidden_units // 2
-    upper, lower = pl.ds(0, half), pl.ds(half, half)
-    down_r, down_l, on_r, on_l = [], [], [], []
-    for c in range(chunks):
-        down_r.append(to_plane(downs.at[0, c], downs.at[1, c], d_s.at[0, c], d_r.at[0, c], right))
-        down_l.append(to_plane(downs.at[0, c], downs.at[2, c], d_s.at[1, c], d_r.at[1, c], left))
-        on_r.append(
-            to_plane(
-                downs.at[1, c, upper], downs.at[3, c, upper], d_s.at[2, c], d_r.at[2, c], right
-            )
-        )
-        on_l.append(
-            to_plane(
-                downs.at[2, c, lower], downs.at[3, c, lower], d_s.at[3, c], d_r.at[3, c], left
-            )
-        )
-
-    def send_down(c):
-        down_r[c].start()
-        down_l[c].start()
+    def chunk_copy(c, source, slot, kind, plane, peer):
+        return to_device(
+            source.at[c], downs.at[slot, c], d_s.at[kind, c], d_r.at[slot, c], plane, peer
+        )
+
+    def chunk_arrived(slot, c):
+        chunk_copy(c, stage, slot, 0, x, me).wait_recv()
+
+    @pl.when(host)
+    def _():
+        for c in range(chunks):
+            for copy in own_down(c, downs.at[0]):
+                copy.wait()
+            chunk_copy(c, downs.at[0], 0, 1, x, sibling).start()
+        for u in range(4):
+            unit_arrived(1, u)
+            onward_unit(u, 1, 1, 2, x, sibling).start()
+        for c in range(2):
+            chunk_copy(c, downs.at[0], 1, 0, partner, me).start()
+
+    @pl.when(guest)
+    def _():
+        for c in range(chunks):
+            for copy in own_down(c, stage):
+                copy.wait()
+            chunk_copy(c, stage, 2, 0, outer, sibling).start()
+        for u in range(4):
+            unit_arrived(2, u)
+            onward_unit(u, 2, 3, 1, partner, me).start()
+            onward_unit(u, 2, 2, 2, x, sibling).start()
+        for c in range(chunks):
+            chunk_arrived(2, c)
+            chunk_copy(c, downs.at[2], 3, 1, partner, me).start()
+            chunk_copy(c, downs.at[2], 2, 2, x, sibling).start()
+        for u in range(4):
+            unit_arrived(3, u)
+            onward_unit(u, 3, 3, 3, x, sibling).start()
 
     def pass_down(c):
-        down_r[c].wait_recv()
-        on_r[c].start()
-        down_l[c].wait_recv()
-        on_l[c].start()
-
-    for copy in own[2:]:
-        copy.wait()
-    send_down(0)
-    gate_r.wait_recv()
-    gate_on.start()
-    up_l.wait_recv()
-    up_on.start()
-    pass_down(0)
-    send_down(1)
-    send_down(2)
+        @pl.when(host)
+        def _():
+            chunk_arrived(1, c)
+            chunk_copy(c, downs.at[1], 1, 2, x, sibling).start()
+
+        @pl.when(guest)
+        def _():
+            chunk_arrived(3, c)
+            chunk_copy(c, downs.at[3], 3, 3, x, sibling).start()
 
     everyone = pl.ds(0, peers - 1)
     to_peer(slot_send.at[everyone], slot_recv.at[everyone], slot_s, slot_r, me).wait_recv()
+    @pl.when(host)
+    def _():
+        for c in range(2, chunks):
+            chunk_copy(c, downs.at[0], 1, 0, partner, me).start()
+
     own_slot.wait()
     tiles = 4
     tile_peers = peers // tiles
@@ -355,17 +424,22 @@
         up_part = dot(rows_in[...], ups[q])
         acts[q] = (gate_part / (1.0 + jnp.exp(-gate_part)) * up_part).astype(BF)
 
-    own[0].wait()
-    own[1].wait()
-    activate(0)
-    up_r.wait_recv()
-    activate(1)
-    gate_l.wait_recv()
-    activate(2)
-
-    gate_on.wait_recv()
-    up_on.wait_recv()
-    activate(3)
+    @pl.when(host)
+    def _():
+        for copy in own:
+            copy.wait()
+        for u in range(4):
+            unit_arrived(2, u)
+            unit_arrived(3, u)
+
+    @pl.when(guest)
+    def _():
+        for u in range(4):
+            unit_arrived(0, u)
+            unit_arrived(1, u)
+
+    for q in range(planes):
+        activate(q)
 
     def combine(j):
         to_peer(
@@ -391,8 +465,16 @@
                 ).start()
 
     def produce(j):
-        on_r[j].wait_recv()
-        on_l[j].wait_recv()
+        @pl.when(host)
+        def _():
+            chunk_arrived(2, j)
+            chunk_arrived(3, j)
+
+        @pl.when(guest)
+        def _():
+            chunk_arrived(0, j)
+            chunk_arrived(1, j)
+
         product = dot(acts[0], downs[0, j])
         for q in range(1, planes):
             product = product + dot(acts[q], downs[q, j])
@@ -406,17 +488,14 @@
                 back_send.at[j, peer], back_recv.at[j, me], back_s.at[j], back_r.at[j], peer
             ).start()
 
-    produce(0)
-    for c in range(1, chunks):
-        pass_down(c)
-        if c + 2 < chunks:
-            send_down(c + 2)
-        if c >= 2:
-            produce(c - 1)
-        if c == 5:
-            combine(0)
-    produce(chunks - 1)
-    for c in range(1, chunks):
+    pass_down(0)
+    for c in range(chunks):
+        if c + 1 < chunks:
+            pass_down(c + 1)
+        produce(c)
+        if c >= 4:
+            combine(c - 4)
+    for c in range(chunks - 4, chunks):
         combine(c)
 
     three = pl.ds(0, planes - 1)
@@ -479,11 +558,24 @@
     later = jnp.max(jnp.where(same, 1, 0), axis=1, keepdims=True)
     place = (asks_down[:, 0:1] // rows) * 8 + later * 4
     at = iota((rows, peers * 8), 1)
-    for copy in (
-        far + near + spread_res + res_on + [gate_r, up_r, up_l, gate_l, gate_on, up_on]
-        + down_r + down_l + on_r + on_l + sq
-    ):
+    for copy in far + near + spread_res + res_on + sq:
         copy.wait_send()
+
+    @pl.when(host)
+    def _():
+        for kind in range(3):
+            for u in range(4):
+                own_unit(u, 0, kind, x, me).wait_send()
+            for c in range(chunks):
+                chunk_copy(c, stage, 0, kind, x, me).wait_send()
+
+    @pl.when(guest)
+    def _():
+        for kind in range(4):
+            for u in range(4):
+                own_unit(u, 0, kind, x, me).wait_send()
+            for c in range(chunks):
+                chunk_copy(c, stage, 0, kind, x, me).wait_send()
 
     @pl.loop(1, peers)
     def _(step):
@@ -551,6 +643,7 @@
                 VMEM((planes, width, units), BF),
                 VMEM((planes, width, units), BF),
                 VMEM((planes, 2 * planes, units, share // 2), BF),
+                VMEM((2 * planes, units, share // 2), BF),
                 VMEM((8, rows), jnp.int32),
                 VMEM((peers, 8, rows), jnp.int32),
                 VMEM((peers, slots, width), BF),
@@ -578,8 +671,8 @@
                 DMA,
                 DMA,
                 DMA,
-                DMA((6,)),
-                DMA((6,)),
+                DMA((4, 4)),
+                DMA((4, 4)),
                 DMA((4, 2 * planes)),
                 DMA((4, 2 * planes)),
                 DMA((2 * planes,)),

time: 165 us -> 154 us (0.933)
  Pallas kernels: 163 us -> 152 us
    pallas_call x1, Pallas kernels: 163 us -> 152 us  [on_device(): pl.pallas_call(functools.partial(layer, planes, peers), out_shape=jax.Sha...]
where the time goes in v5:
time: 154 us; the launch traced here: 153 us
  Pallas kernels  152 us (99%)
  local copies, waits for them, and re-layouts  1.57 us (1%)
    pallas_call x1, Pallas kernels, on_device(): pl.pallas_call(functools.partial(layer, planes, peers), out_shape=jax.Sha...  152 us

profile of v5, /device:TPU:1, one launch (start us, length us, event | category | flops | bytes accessed | tf_op | source)
XLA Modules:
  0.0 153.5 jit_solution(15779028530614975373)
XLA Ops:
  0.0 151.9 %shard_map.109 = bf16[128,512]{1,0:T(8,128)(2,1)} custom-call(bf16[128,512]{1,0:T(8,128)(2,1)} %attn_hbm.1, bf16[512,2048]{1,0:T(8,128)(2,1)} %proj_hbm.1, bf16[128,2048]{1,0:T(8,128)(2,1)} %hidden_hbm.1, bf16[2048]{0:T(1024)(128)(2,1)} %gain_hbm.1, bf16[64,2048]{1,0:T(8,128)(2,1)} %bitcast.3, s32[8,128]{1,0:T(8,128)} %bitcast.4, ...), custom_call_target="tpu_custom_call" | custom-call | tf_op jit(solution)/shard_map/pallas_call | solution.py:622
  151.9 1.6 %copy.13 = bf16[128,512]{1,0:T(8,128)(2,1)} copy(bf16[128,512]{1,0:T(8,128)(2,1)} %shard_map.109) | data formatting | bytes 262144

commit v6 on v5

--- a/solution.py
+++ b/solution.py
@@ -202,20 +202,29 @@
     for j in range(planes):
         part[j] = dot(attn_ref[...], proj_ref[:, j * share : (j + 1) * share])
     top, bottom = pl.ds(0, rows // 2), pl.ds(rows // 2, rows // 2)
-    far_send[...] = part[lax.rem(x + 2, planes)].astype(BF)
+    wing = share // 2
+    wings = [pl.ds(0, wing), pl.ds(wing, wing)]
+    for h in range(2):
+        far_send[h] = part[lax.rem(x + 2, planes), :, wings[h]].astype(BF)
 
     pl.semaphore_wait(barrier, planes - 1 + 1 + peers - 1)
 
     far = [
-        to_plane(far_send.at[top], far_recv.at[0], att_s.at[0], att_r.at[0], right),
-        to_plane(far_send.at[bottom], far_recv.at[1], att_s.at[1], att_r.at[1], left),
+        [
+            to_plane(far_send.at[h, top], far_recv.at[h, 0], att_s.at[h, 0], att_r.at[h, 0], right),
+            to_plane(
+                far_send.at[h, bottom], far_recv.at[h, 1], att_s.at[h, 1], att_r.at[h, 1], left
+            ),
+        ]
+        for h in range(2)
     ]
-    for copy in far:
+    for copy in far[0] + far[1]:
         copy.start()
 
-    fill = width // 16
-    middle = width // 2
-    units_of = [(gates, gate_hbm, 0), (gates, gate_hbm, middle), (ups, up_hbm, 0), (ups, up_hbm, middle)]
+    middle = width // 4
+    units_of = [(gates, gate_hbm, first) for first in range(0, width, middle)]
+    units_of += [(ups, up_hbm, first) for first in range(0, width, middle)]
+    unit_count = len(units_of)
 
     def unit_view(slot, u):
         buffer, _, first = units_of[u]
@@ -240,68 +249,93 @@
     def unit_arrived(slot, u):
         own_unit(u, slot, 0, x, me).wait_recv()
 
-    def send_units(first, count, later):
+    def send_rows(phase):
+        def spans(marks):
+            marks = (0,) + marks + (unit_count * middle,)
+            first, last = marks[phase], marks[phase + 1]
+            while first < last:
+                count = min(last, first // middle * middle + middle) - first
+                yield first // middle, first % middle, count
+                first += count
+
         @pl.when(host)
         def _():
-            own_unit(0, 1, 0, partner, me, first, count).start()
-            for u in range(1, 4 if later else 1):
-                own_unit(u, 1, 0, partner, me).start()
+            for u, first, count in spans((128, 256, 384)):
+                own_unit(u, 1, 0, partner, me, first, count).start()
 
         @pl.when(guest)
         def _():
-            own_unit(0, 2, 0, outer, sibling, first, count).start()
-            for u in range(1, 4 if later else 1):
-                own_unit(u, 2, 0, outer, sibling).start()
-
-    send_units(0, fill, False)
+            for u, first, count in spans((128, 256, 384)):
+                own_unit(u, 2, 0, outer, sibling, first, count).start()
+
+    send_rows(0)
+
+    near = []
+    for h in range(2):
+        for copy in far[h]:
+            copy.wait_recv()
+        wing_at = wings[h]
+        near_send[h, 0] = part[right, :, wing_at].astype(BF)
+        near_send[h, 1] = part[left, :, wing_at].astype(BF)
+        near_send[h, 0, top] = (part[right, top, wing_at] + far_recv[h, 0].astype(F32)).astype(BF)
+        near_send[h, 1, bottom] = (part[left, bottom, wing_at] + far_recv[h, 1].astype(F32)).astype(BF)
+        near.append(
+            [
+                to_plane(
+                    near_send.at[h, 0], near_recv.at[h, 0], att_s.at[h, 2], att_r.at[h, 2], right
+                ),
+                to_plane(
+                    near_send.at[h, 1], near_recv.at[h, 1], att_s.at[h, 3], att_r.at[h, 3], left
+                ),
+            ]
+        )
+        for copy in near[h]:
+            copy.start()
+    send_rows(1)
 
     @pl.loop(1, peers)
     def _(step):
         to_peer(ask_send, ask_recv.at[me], ask_s, ask_r, peer_at(step)).start()
 
-    for copy in far:
-        copy.wait_recv()
-    near_send[0] = part[right].astype(BF)
-    near_send[1] = part[left].astype(BF)
-    near_send[0, top] = (part[right, top] + far_recv[0].astype(F32)).astype(BF)
-    near_send[1, bottom] = (part[left, bottom] + far_recv[1].astype(F32)).astype(BF)
-    near = [
-        to_plane(near_send.at[0], near_recv.at[0], att_s.at[2], att_r.at[2], right),
-        to_plane(near_send.at[1], near_recv.at[1], att_s.at[3], att_r.at[3], left),
-    ]
-    for copy in near:
-        copy.start()
-    send_units(fill, fill, False)
     for copy in inputs[2:7]:
         copy.wait()
-    for copy in near:
-        copy.wait_recv()
-    mine = pl.ds(pl.multiple_of(x * share, share), share)
-    attention = part[x] + near_recv[0].astype(F32) + near_recv[1].astype(F32)
-    res[x] = (hidden_ref[:, mine].astype(F32) + attention).astype(BF)
-    spread_res = [
-        to_plane(res.at[x], res.at[x], res_s.at[0], res_r.at[0], right),
-        to_plane(res.at[x], res.at[x], res_s.at[1], res_r.at[1], left),
-    ]
-    for copy in spread_res:
-        copy.start()
-    send_units(2 * fill, fill, False)
-    res_on = [
-        to_plane(res.at[left, top], res.at[left, top], res_s.at[2], res_r.at[2], right),
-        to_plane(res.at[right, bottom], res.at[right, bottom], res_s.at[3], res_r.at[3], left),
-    ]
-    for copy, onward in zip(spread_res, res_on):
-        copy.wait_recv()
-        onward.start()
-    send_units(3 * fill, middle - 3 * fill, True)
+    spread_res, res_on = [], []
+    for h in range(2):
+        for copy in near[h]:
+            copy.wait_recv()
+        mine = pl.ds(pl.multiple_of(x * share + h * wing, wing), wing)
+        attention = part[x, :, wings[h]] + near_recv[h, 0].astype(F32) + near_recv[h, 1].astype(F32)
+        res[x, :, wings[h]] = (hidden_ref[:, mine].astype(F32) + attention).astype(BF)
+        ours = res.at[x, :, wings[h]]
+        spread_res.append(
+            [
+                to_plane(ours, ours, res_s.at[h, 0], res_r.at[h, 0], right),
+                to_plane(ours, ours, res_s.at[h, 1], res_r.at[h, 1], left),
+            ]
+        )
+        for copy in spread_res[h]:
+            copy.start()
+    send_rows(2)
+    for h in range(2):
+        from_left, from_right = res.at[left, top, wings[h]], res.at[right, bottom, wings[h]]
+        res_on.append(
+            [
+                to_plane(from_left, from_left, res_s.at[h, 2], res_r.at[h, 2], right),
+                to_plane(from_right, from_right, res_s.at[h, 3], res_r.at[h, 3], left),
+            ]
+        )
+        for copy, onward in zip(spread_res[h], res_on[h]):
+            copy.wait_recv()
+            onward.start()
+    send_rows(3)
 
     @pl.when(host)
     def _():
-        for u in range(4):
+        for u in range(unit_count):
             own_unit(u, 0, 1, x, sibling).start()
 
 
-    for copy in res_on:
+    for copy in res_on[0] + res_on[1]:
         copy.wait_recv()
     square = jnp.zeros((rows, 1), F32)
     for j in range(planes):
@@ -346,12 +380,17 @@
         chosen = dot(pick, normed[j]).astype(BF)
         slot_send[:, :, j * share : (j + 1) * share] = chosen.reshape(peers, slots, share)
 
-    @pl.loop(1, peers)
-    def _(step):
-        peer = peer_at(step)
-        to_peer(slot_send.at[peer], slot_recv.at[me], slot_s, slot_r, peer).start()
-
-    own_slot = pltpu.make_async_copy(slot_send.at[me], slot_recv.at[me], own_sem.at[2 + 2 * chunks])
+    side = peers // 2
+    for h in range(2):
+
+        @pl.loop(1 - h, side)
+        def _(k):
+            peer = peer_at(2 * k + h)
+            to_peer(
+                slot_send.at[peer], slot_recv.at[k + h * side], slot_s, slot_r.at[h], peer
+            ).start()
+
+    own_slot = pltpu.make_async_copy(slot_send.at[me], slot_recv.at[0], own_sem.at[2 + 2 * chunks])
     own_slot.start()
 
     def chunk_copy(c, source, slot, kind, plane, peer):
@@ -368,10 +407,10 @@
             for copy in own_down(c, downs.at[0]):
                 copy.wait()
             chunk_copy(c, downs.at[0], 0, 1, x, sibling).start()
-        for u in range(4):
+        for u in range(unit_count):
             unit_arrived(1, u)
             onward_unit(u, 1, 1, 2, x, sibling).start()
-        for c in range(2):
+        for c in range(1):
             chunk_copy(c, downs.at[0], 1, 0, partner, me).start()
 
     @pl.when(guest)
@@ -380,7 +419,7 @@
             for copy in own_down(c, stage):
                 copy.wait()
             chunk_copy(c, stage, 2, 0, outer, sibling).start()
-        for u in range(4):
+        for u in range(unit_count):
             unit_arrived(2, u)
             onward_unit(u, 2, 3, 1, partner, me).start()
             onward_unit(u, 2, 2, 2, x, sibling).start()
@@ -388,10 +427,6 @@
             chunk_arrived(2, c)
             chunk_copy(c, downs.at[2], 3, 1, partner, me).start()
             chunk_copy(c, downs.at[2], 2, 2, x, sibling).start()
-        for u in range(4):
-            unit_arrived(3, u)
-            onward_unit(u, 3, 3, 3, x, sibling).start()
-
     def pass_down(c):
         @pl.when(host)
         def _():
@@ -404,42 +439,67 @@
             chunk_copy(c, downs.at[3], 3, 3, x, sibling).start()
 
     everyone = pl.ds(0, peers - 1)
-    to_peer(slot_send.at[everyone], slot_recv.at[everyone], slot_s, slot_r, me).wait_recv()
-    @pl.when(host)
-    def _():
-        for c in range(2, chunks):
-            chunk_copy(c, downs.at[0], 1, 0, partner, me).start()
+    side_rows = side * slots
+
+    def take_rows(h):
+        count = pl.ds(0, side - 1 if h == 0 else side)
+        to_peer(slot_send.at[count], slot_recv.at[count], slot_s, slot_r.at[h], me).wait_recv()
+        half_side = side // 2
+        for t in range(2):
+            first = h * side + t * half_side
+            rows_in[first * slots : (first + half_side) * slots] = slot_recv[
+                first : first + half_side
+            ].reshape(half_side * slots, width)
+
+    def activate(q, h):
+        there = slice(h * side_rows, (h + 1) * side_rows)
+        gate_part = dot(rows_in[there], gates[q])
+        up_part = dot(rows_in[there], ups[q])
+        acts[q, there] = (gate_part / (1.0 + jnp.exp(-gate_part)) * up_part).astype(BF)
 
     own_slot.wait()
-    tiles = 4
-    tile_peers = peers // tiles
-    tile_rows = tile_peers * slots
-    for t in range(tiles):
-        rows_in[t * tile_rows : (t + 1) * tile_rows] = slot_recv[
-            t * tile_peers : (t + 1) * tile_peers
-        ].reshape(tile_rows, width)
-
-    def activate(q):
-        gate_part = dot(rows_in[...], gates[q])
-        up_part = dot(rows_in[...], ups[q])
-        acts[q] = (gate_part / (1.0 + jnp.exp(-gate_part)) * up_part).astype(BF)
+    take_rows(0)
 
     @pl.when(host)
     def _():
         for copy in own:
             copy.wait()
-        for u in range(4):
+
+    @pl.when(guest)
+    def _():
+        for u in range(unit_count):
+            unit_arrived(0, u)
+
+    activate(0, 0)
+
+    @pl.when(host)
+    def _():
+        for u in range(unit_count):
             unit_arrived(2, u)
+
+    activate(2, 0)
+
+    @pl.when(guest)
+    def _():
+        for u in range(unit_count):
+            unit_arrived(1, u)
+
+    activate(1, 0)
+
+    @pl.when(host)
+    def _():
+        for u in range(unit_count):
             unit_arrived(3, u)
+        for c in range(1, chunks):
+            chunk_copy(c, downs.at[0], 1, 0, partner, me).start()
 
     @pl.when(guest)
     def _():
-        for u in range(4):
-            unit_arrived(0, u)
-            unit_arrived(1, u)
-
-    for q in range(planes):
-        activate(q)
+        for u in range(unit_count):
+            unit_arrived(3, u)
+            onward_unit(u, 3, 3, 3, x, sibling).start()
+
+    activate(3, 0)
 
     def combine(j):
         to_peer(
@@ -464,35 +524,50 @@
                     mix_send.at[at, plane], mix_recv.at[slot, at], mix_s, mix_r, plane
                 ).start()
 
-    def produce(j):
+    def chunk_ready(c):
         @pl.when(host)
         def _():
-            chunk_arrived(2, j)
-            chunk_arrived(3, j)
+            chunk_arrived(2, c)
+            chunk_arrived(3, c)
 
         @pl.when(guest)
         def _():
-            chunk_arrived(0, j)
-            chunk_arrived(1, j)
-
-        product = dot(acts[0], downs[0, j])
+            chunk_arrived(0, c)
+            chunk_arrived(1, c)
+
+    def produce(j, h):
+        there = slice(h * side_rows, (h + 1) * side_rows)
+        product = dot(acts[0, there], downs[0, j])
         for q in range(1, planes):
-            product = product + dot(acts[q], downs[q, j])
-        back_send[j] = product.astype(BF).reshape(peers, slots, 2 * piece)
-        back_recv[j, me] = back_send[j, me]
-
-        @pl.loop(1, peers)
-        def _(step):
-            peer = peer_at(step)
+            product = product + dot(acts[q, there], downs[q, j])
+        back_send[j, h * side : (h + 1) * side] = product.astype(BF).reshape(side, slots, 2 * piece)
+        if h == 0:
+            back_recv[j, me] = back_send[j, 0]
+
+        @pl.loop(1 - h, side)
+        def _(k):
             to_peer(
-                back_send.at[j, peer], back_recv.at[j, me], back_s.at[j], back_r.at[j], peer
+                back_send.at[j, k + h * side],
+                back_recv.at[j, me],
+                back_s.at[j],
+                back_r.at[j],
+                peer_at(peers - 2 * k - h),
             ).start()
 
     pass_down(0)
-    for c in range(chunks):
+    chunk_ready(0)
+    produce(0, 0)
+    take_rows(1)
+    for q in range(planes):
+        activate(q, 1)
+    produce(0, 1)
+    pass_down(1)
+    for c in range(1, chunks):
         if c + 1 < chunks:
             pass_down(c + 1)
-        produce(c)
+        chunk_ready(c)
+        produce(c, 0)
+        produce(c, 1)
         if c >= 4:
             combine(c - 4)
     for c in range(chunks - 4, chunks):
@@ -558,13 +633,14 @@
     later = jnp.max(jnp.where(same, 1, 0), axis=1, keepdims=True)
     place = (asks_down[:, 0:1] // rows) * 8 + later * 4
     at = iota((rows, peers * 8), 1)
-    for copy in far + near + spread_res + res_on + sq:
+    att = far + near + spread_res + res_on
+    for copy in sum(att, []) + sq:
         copy.wait_send()
 
     @pl.when(host)
     def _():
         for kind in range(3):
-            for u in range(4):
+            for u in range(unit_count):
                 own_unit(u, 0, kind, x, me).wait_send()
             for c in range(chunks):
                 chunk_copy(c, stage, 0, kind, x, me).wait_send()
@@ -572,7 +648,7 @@
     @pl.when(guest)
     def _():
         for kind in range(4):
-            for u in range(4):
+            for u in range(unit_count):
                 own_unit(u, 0, kind, x, me).wait_send()
             for c in range(chunks):
                 chunk_copy(c, stage, 0, kind, x, me).wait_send()
@@ -634,10 +710,10 @@
                 VMEM((share,), BF),
                 VMEM((1, rows), jnp.int32),
                 VMEM((planes, rows, share), F32),
-                VMEM((rows, share), BF),
-                VMEM((2, rows // 2, share), BF),
-                VMEM((2, rows, share), BF),
-                VMEM((2, rows, share), BF),
+                VMEM((2, rows, share // 2), BF),
+                VMEM((2, 2, rows // 2, share // 2), BF),
+                VMEM((2, 2, rows, share // 2), BF),
+                VMEM((2, 2, rows, share // 2), BF),
                 VMEM((planes, rows, share), BF),
                 VMEM((planes, rows, share), BF),
                 VMEM((planes, width, units), BF),
@@ -663,16 +739,16 @@
                 VMEM((rows, peers * slots), BF),
                 DMA((8,)),
                 DMA((3 + 4 * planes,)),
-                DMA((4,)),
-                DMA((4,)),
-                DMA((4,)),
-                DMA((4,)),
+                DMA((2, 4)),
+                DMA((2, 4)),
+                DMA((2, 4)),
+                DMA((2, 4)),
                 DMA,
                 DMA,
                 DMA,
-                DMA,
-                DMA((4, 4)),
-                DMA((4, 4)),
+                DMA((2,)),
+                DMA((4, 8)),
+                DMA((4, 8)),
                 DMA((4, 2 * planes)),
                 DMA((4, 2 * planes)),
                 DMA((2 * planes,)),

time: 154 us -> 145 us (0.942)
  Pallas kernels: 152 us -> 144 us
    pallas_call x1, Pallas kernels: 152 us -> 144 us  [on_device(): pl.pallas_call(functools.partial(layer, planes, peers), out_shape=jax.Sha...]
where the time goes in v6:
time: 145 us
  Pallas kernels  144 us (99%)
  local copies, waits for them, and re-layouts  1.57 us (1%)
    pallas_call x1, Pallas kernels, on_device(): pl.pallas_call(functools.partial(layer, planes, peers), out_shape=jax.Sha...  144 us

profile of v6, /device:TPU:1, one launch (start us, length us, event | category | flops | bytes accessed | tf_op | source)
XLA Modules:
  0.0 145.3 jit_solution(435739244805669901)
XLA Ops:
  0.0 143.7 %shard_map.109 = bf16[128,512]{1,0:T(8,128)(2,1)} custom-call(bf16[128,512]{1,0:T(8,128)(2,1)} %attn_hbm.1, bf16[512,2048]{1,0:T(8,128)(2,1)} %proj_hbm.1, bf16[128,2048]{1,0:T(8,128)(2,1)} %hidden_hbm.1, bf16[2048]{0:T(1024)(128)(2,1)} %gain_hbm.1, bf16[64,2048]{1,0:T(8,128)(2,1)} %bitcast.3, s32[8,128]{1,0:T(8,128)} %bitcast.4, ...), custom_call_target="tpu_custom_call" | custom-call | tf_op jit(solution)/shard_map/pallas_call | solution.py:698
  143.7 1.6 %copy.13 = bf16[128,512]{1,0:T(8,128)(2,1)} copy(bf16[128,512]{1,0:T(8,128)(2,1)} %shard_map.109) | data formatting | bytes 262144

commit v7 on v6

--- a/solution.py
+++ b/solution.py
@@ -67,8 +67,11 @@
     mix_send,
     mix_recv,
     total,
-    sq_send,
-    sq_recv,
+    squares,
+    pick_ref,
+    taken_ref,
+    pack_pick,
+    out_pick,
     pack_send,
     pack_recv,
     high,
@@ -91,8 +94,6 @@
     back_r,
     mix_s,
     mix_r,
-    sq_s,
-    sq_r,
     pack_s,
     pack_r,
 ):
@@ -299,6 +300,28 @@
 
     for copy in inputs[2:7]:
         copy.wait()
+
+    experts = peers
+    named = jnp.zeros((rows, experts), jnp.bool_)
+    which = iota((rows, experts), 1)
+    routed = jnp.transpose(routes_ref[...].astype(F32)).astype(jnp.int32)
+    for k in range(routed.shape[1]):
+        named = named | (routed[:, k : k + 1] == which)
+    named_f = jnp.where(named, 1.0, 0.0).astype(F32)
+    before = jnp.where(iota((rows, rows), 1) < iota((rows, rows), 0), 1.0, 0.0).astype(BF)
+    rank = dot(before, named_f.astype(BF))
+    wide = jnp.where(
+        iota((experts, all_slots), 1) // (2 * slots) * 2 + active == iota((experts, all_slots), 0),
+        1.0,
+        0.0,
+    ).astype(BF)
+    wide_rank = dot(rank.astype(BF), wide)
+    wide_named = dot(named_f.astype(BF), wide)
+    turn = (iota((rows, all_slots), 1) % (2 * slots) + lax.rem(x, 2) * 2 * slots).astype(F32)
+    taken_f = jnp.where((wide_named > 0.5) & (wide_rank == turn), 1.0, 0.0).astype(F32)
+    taken_ref[...] = taken_f.astype(BF)
+    pick_ref[...] = jnp.transpose(taken_f).astype(BF)
+
     spread_res, res_on = [], []
     for h in range(2):
         for copy in near[h]:
@@ -342,40 +365,11 @@
         floats = res[j].astype(F32)
         square = square + jnp.sum(floats * floats, axis=1, keepdims=True)
     inverse = lax.rsqrt(square / width + epsilon)
-    experts = peers
-    logits = jnp.zeros((rows, experts), F32)
     for j in range(planes):
         cols = slice(j * share, (j + 1) * share)
         gain = gain_ref[cols].astype(F32).reshape(1, share)
-        scaled = (res[j].astype(F32) * inverse * gain).astype(BF)
-        normed[j] = scaled
-        logits = logits + lax.dot_general(
-            scaled, router_ref[:, cols], (((1,), (1,)), ((), ())), preferred_element_type=F32
-        )
-    named = jnp.zeros((rows, experts), jnp.bool_)
-    which = iota((rows, experts), 1)
-    routed = jnp.transpose(routes_ref[...].astype(F32)).astype(jnp.int32)
-    for k in range(routed.shape[1]):
-        named = named | (routed[:, k : k + 1] == which)
-    named_f = jnp.where(named, 1.0, 0.0).astype(F32)
-    powers = jnp.where(named, jnp.exp(logits), 0.0)
-    weights = powers / jnp.sum(powers, axis=1, keepdims=True)
-    before = jnp.where(iota((rows, rows), 1) < iota((rows, rows), 0), 1.0, 0.0).astype(BF)
-    rank = dot(before, named_f.astype(BF))
-    wide = jnp.where(
-        iota((experts, all_slots), 1) // (2 * slots) * 2 + active == iota((experts, all_slots), 0),
-        1.0,
-        0.0,
-    ).astype(BF)
-    wide_rank = dot(rank.astype(BF), wide)
-    wide_named = dot(named_f.astype(BF), wide)
-    turn = (iota((rows, all_slots), 1) % (2 * slots) + lax.rem(x, 2) * 2 * slots).astype(F32)
-    taken = (wide_named > 0.5) & (wide_rank == turn)
-    weights_high = weights.astype(BF)
-    weights_low = (weights - weights_high.astype(F32)).astype(BF)
-    high[...] = jnp.where(taken, dot(weights_high, wide), 0.0).astype(BF)
-    low[...] = jnp.where(taken, dot(weights_low, wide), 0.0).astype(BF)
-    pick = jnp.transpose(jnp.where(taken, 1.0, 0.0).astype(F32)).astype(BF)
+        normed[j] = (res[j].astype(F32) * inverse * gain).astype(BF)
+    pick = pick_ref[...]
     for j in range(planes):
         chosen = dot(pick, normed[j]).astype(BF)
         slot_send[:, :, j * share : (j + 1) * share] = chosen.reshape(peers, slots, share)
@@ -392,6 +386,20 @@
 
     own_slot = pltpu.make_async_copy(slot_send.at[me], slot_recv.at[0], own_sem.at[2 + 2 * chunks])
     own_slot.start()
+
+    logits = jnp.zeros((rows, experts), F32)
+    for j in range(planes):
+        cols = slice(j * share, (j + 1) * share)
+        logits = logits + lax.dot_general(
+            normed[j], router_ref[:, cols], (((1,), (1,)), ((), ())), preferred_element_type=F32
+        )
+    powers = jnp.where(named, jnp.exp(logits), 0.0)
+    weights = powers / jnp.sum(powers, axis=1, keepdims=True)
+    weights_high = weights.astype(BF)
+    weights_low = (weights - weights_high.astype(F32)).astype(BF)
+    taken = taken_ref[...].astype(F32) > 0.5
+    high[...] = jnp.where(taken, dot(weights_high, wide), 0.0).astype(BF)
+    low[...] = jnp.where(taken, dot(weights_low, wide), 0.0).astype(BF)
 
     def chunk_copy(c, source, slot, kind, plane, peer):
         return to_device(
@@ -501,28 +509,44 @@
 
     activate(3, 0)
 
-    def combine(j):
-        to_peer(
-            back_send.at[j, everyone], back_recv.at[j, everyone], back_s.at[j], back_r.at[j], me
-        ).wait_recv()
-        back = back_recv[j].reshape(all_slots, 2 * piece)
+    groups = [[0], [1]] + [[c, c + 1] for c in range(2, chunks - 2, 2)] + [[chunks - 2], [chunks - 1]]
+    group_of = {c: g for g, group in enumerate(groups) for c in group}
+
+    def back_copy(g, here, there, peer):
+        first = groups[g][0]
+        if len(groups[g]) == 1:
+            src, dst = back_send.at[first // 2, here, first % 2], back_recv.at[first // 2, there, first % 2]
+        else:
+            src, dst = back_send.at[first // 2, here], back_recv.at[first // 2, there]
+        return to_peer(src, dst, back_s.at[g], back_r.at[g], peer)
+
+    def mix_copy(c, d):
+        return to_plane(
+            mix_send.at[c], mix_recv.at[c, d - 1], mix_s.at[c], mix_r.at[c], lax.rem(x + d, planes)
+        )
+
+    def combine(c):
+        if groups[group_of[c]][0] == c:
+            back_copy(group_of[c], everyone, everyone, me).wait_recv()
+        back = back_recv[c // 2, :, c % 2].reshape(all_slots, 2 * piece)
         mixed = dot(high[...], back) + dot(low[...], back)
-        at = j // 2
-        for i in range(2):
-            plane = j % 2 * 2 + i
-            part_of = mixed[:, i * piece : (i + 1) * piece]
-            mix_send[at, plane] = part_of.astype(BF)
-
-            @pl.when(x == plane)
-            def _():
-                total[:, at * piece : (at + 1) * piece] = part_of
-
-            @pl.when(x != plane)
-            def _():
-                slot = lax.rem(x - plane + planes, planes) - 1
-                to_plane(
-                    mix_send.at[at, plane], mix_recv.at[slot, at], mix_s, mix_r, plane
-                ).start()
+        mix_send[c] = mixed.astype(BF)
+        total[c] = mixed
+        for d in range(1, planes):
+            mix_copy(c, d).start()
+
+    three = pl.ds(0, planes - 1)
+
+    def finish(c):
+        to_plane(mix_recv.at[c, three], mix_recv.at[c, three], mix_s.at[c], mix_r.at[c], x).wait_recv()
+        at = slice(c // 2 * piece, (c // 2 + 1) * piece)
+        first = c % 2 * 2
+        whole = total[c] + jnp.concatenate([res[first, :, at], res[first + 1, :, at]], axis=1).astype(F32)
+        for d in range(planes - 1):
+            whole = whole + mix_recv[c, d].astype(F32)
+        total[c] = whole
+        added = whole[:, :piece] * whole[:, :piece] + whole[:, piece:] * whole[:, piece:]
+        squares[...] = added if c == 0 else squares[...] + added
 
     def chunk_ready(c):
         @pl.when(host)
@@ -540,59 +564,40 @@
         product = dot(acts[0, there], downs[0, j])
         for q in range(1, planes):
             product = product + dot(acts[q, there], downs[q, j])
-        back_send[j, h * side : (h + 1) * side] = product.astype(BF).reshape(side, slots, 2 * piece)
+        block = product.astype(BF).reshape(side, slots, 2 * piece)
+        back_send[j // 2, h * side : (h + 1) * side, j % 2] = block
         if h == 0:
-            back_recv[j, me] = back_send[j, 0]
-
+            back_recv[j // 2, me, j % 2] = block[0]
+
+    def send_back(g, h):
         @pl.loop(1 - h, side)
         def _(k):
-            to_peer(
-                back_send.at[j, k + h * side],
-                back_recv.at[j, me],
-                back_s.at[j],
-                back_r.at[j],
-                peer_at(peers - 2 * k - h),
-            ).start()
+            back_copy(g, k + h * side, me, peer_at(peers - 2 * k - h)).start()
 
     pass_down(0)
     chunk_ready(0)
     produce(0, 0)
+    send_back(0, 0)
     take_rows(1)
     for q in range(planes):
         activate(q, 1)
     produce(0, 1)
+    send_back(0, 1)
     pass_down(1)
     for c in range(1, chunks):
         if c + 1 < chunks:
             pass_down(c + 1)
         chunk_ready(c)
-        produce(c, 0)
-        produce(c, 1)
+        g = group_of[c]
+        last = groups[g][-1] == c
+        for h in range(2):
+            produce(c, h)
+            if last:
+                send_back(g, h)
         if c >= 4:
             combine(c - 4)
-    for c in range(chunks - 4, chunks):
-        combine(c)
-
-    three = pl.ds(0, planes - 1)
-    to_plane(mix_recv.at[three], mix_recv.at[three], mix_s, mix_r, x).wait_recv()
-    mixture = [total[:, j * piece : (j + 1) * piece] for j in range(planes)]
-    for j in range(planes):
-        for d in range(planes - 1):
-            mixture[j] = mixture[j] + mix_recv[d, j].astype(F32)
-    whole = jnp.concatenate(mixture, axis=1) + res[x].astype(F32)
-    total[...] = whole
-    squares = jnp.zeros((rows, 128), F32)
-    for c in range(share // 128):
-        part_of = whole[:, c * 128 : (c + 1) * 128]
-        squares = squares + part_of * part_of
-    row_sum = jnp.sum(jnp.transpose(squares), axis=0, keepdims=True)
-    sq_send[...] = jnp.broadcast_to(row_sum, sq_send.shape)
-    sq = [
-        to_plane(sq_send, sq_recv.at[d - 1], sq_s.at[d - 1], sq_r.at[d - 1], lax.rem(x + d, planes))
-        for d in range(1, planes)
-    ]
-    for copy in sq:
-        copy.start()
+        if c >= 5:
+            finish(c - 5)
 
     to_peer(ask_recv.at[everyone], ask_recv.at[everyone], ask_s, ask_r, me).wait_recv()
     ask_recv[me] = ask_send[...]
@@ -604,28 +609,9 @@
     line = iota((peers * 8, 1), 0) % 8
     request = jnp.where(line < 4, first, second)
     local = jnp.sum(jnp.where(lanes == request, asked % rows, 0), axis=1, keepdims=True)
-    wanted = lanes == local
-
-    for copy in sq:
-        copy.wait_recv()
-    sums = sq_send[...]
-    for d in range(planes - 1):
-        sums = sums + sq_recv[d]
-    column = jnp.transpose(jnp.broadcast_to(sums[0:1], (rows, rows)))[:, 0:1]
-    scale = lax.rsqrt(column / width + epsilon)
-    last_gain = last_gain_ref[...].astype(F32).reshape(1, share)
-    result = (total[...] * scale * last_gain).astype(BF)
-    packed = jnp.zeros((peers * 8, 128), F32)
-    for c in range(4):
-        chooser = jnp.where(wanted & (line % 4 == c), 1.0, 0.0).astype(BF)
-        packed = packed + dot(chooser, result[:, c * 128 : (c + 1) * 128])
-    pack_send[...] = packed.astype(BF).reshape(peers, 8, 128)
-    pack_recv[me] = pack_send[me]
-
-    @pl.loop(1, peers)
-    def _(step):
-        peer = peer_at(step)
-        to_peer(pack_send.at[peer], pack_recv.at[me], pack_s, pack_r, peer).start()
+    for c in range(planes):
+        chooser = (lanes == local) & (line % 4 == c)
+        pack_pick[c] = jnp.where(chooser, 1.0, 0.0).astype(BF)
 
     asks = jnp.broadcast_to(source_ref[...], (rows, rows))
     asks_down = jnp.transpose(asks.astype(F32)).astype(jnp.int32)
@@ -633,8 +619,37 @@
     later = jnp.max(jnp.where(same, 1, 0), axis=1, keepdims=True)
     place = (asks_down[:, 0:1] // rows) * 8 + later * 4
     at = iota((rows, peers * 8), 1)
+    for c in range(planes):
+        out_pick[c] = jnp.where(at == place + c, 1.0, 0.0).astype(BF)
+
+    for c in range(chunks - 4, chunks):
+        combine(c)
+        finish(c - 1)
+    finish(chunks - 1)
+    square = jnp.sum(squares[...], axis=1, keepdims=True)
+    scale = lax.rsqrt(square / width + epsilon)
+    packed = jnp.zeros((peers * 8, piece), F32)
+    own_half = pl.ds(pl.multiple_of(lax.rem(x, 2) * piece, piece), piece)
+    for c in range(planes):
+        gain = last_gain_ref[c * piece : (c + 1) * piece].astype(F32).reshape(1, piece)
+        result = (total[2 * c + active, :, own_half] * scale * gain).astype(BF)
+        packed = packed + dot(pack_pick[c], result)
+    pack_send[...] = packed.astype(BF).reshape(peers, 8, piece)
+    pack_recv[me] = pack_send[me]
+
+    def send_pack(step):
+        peer = peer_at(step)
+        to_peer(pack_send.at[peer], pack_recv.at[me], pack_s, pack_r, peer).start()
+
+    send_pack(side)
+
+    @pl.loop(1, side)
+    def _(k):
+        send_pack(side - k)
+        send_pack(side + k)
+
     att = far + near + spread_res + res_on
-    for copy in sum(att, []) + sq:
+    for copy in sum(att, []):
         copy.wait_send()
 
     @pl.when(host)
@@ -658,16 +673,15 @@
         to_peer(ask_send, ask_recv.at[me], ask_s, ask_r, me).wait_send()
 
     to_peer(slot_send.at[everyone], slot_recv.at[everyone], slot_s, slot_r, me).wait_send()
-    for j in range(chunks):
-        to_peer(
-            back_send.at[j, everyone], back_recv.at[j, everyone], back_s.at[j], back_r.at[j], me
-        ).wait_send()
-    to_plane(mix_send.at[:, three], mix_recv.at[three], mix_s, mix_r, x).wait_send()
+    for g in range(len(groups)):
+        back_copy(g, everyone, everyone, me).wait_send()
+    for c in range(chunks):
+        for d in range(1, planes):
+            mix_copy(c, d).wait_send()
     to_peer(pack_send.at[everyone], pack_recv.at[everyone], pack_s, pack_r, me).wait_recv()
     landed = pack_recv[...].reshape(peers * 8, 128)
-    for c in range(4):
-        chooser = jnp.where(at == place + c, 1.0, 0.0).astype(BF)
-        out_ref[:, c * 128 : (c + 1) * 128] = dot(chooser, landed).astype(BF)
+    for c in range(planes):
+        out_ref[:, c * piece : (c + 1) * piece] = dot(out_pick[c], landed).astype(BF)
 
     to_peer(pack_send.at[everyone], pack_recv.at[everyone], pack_s, pack_r, me).wait_send()
 
@@ -726,13 +740,16 @@
                 VMEM((peers, slots, width), BF),
                 VMEM((peers * slots, width), BF),
                 VMEM((planes, peers * slots, units), BF),
-                VMEM((2 * planes, peers, slots, share // 2), BF),
-                VMEM((2 * planes, peers, slots, share // 2), BF),
-                VMEM((planes, planes, rows, share // planes), BF),
-                VMEM((planes - 1, planes, rows, share // planes), BF),
-                VMEM((rows, share), F32),
-                VMEM((8, rows), F32),
-                VMEM((planes - 1, 8, rows), F32),
+                VMEM((planes, peers, 2, slots, share // 2), BF),
+                VMEM((planes, peers, 2, slots, share // 2), BF),
+                VMEM((2 * planes, rows, share // 2), BF),
+                VMEM((2 * planes, planes - 1, rows, share // 2), BF),
+                VMEM((2 * planes, rows, share // 2), F32),
+                VMEM((rows, share // planes), F32),
+                VMEM((peers * slots, rows), BF),
+                VMEM((rows, peers * slots), BF),
+                VMEM((planes, peers * 8, rows), BF),
+                VMEM((planes, rows, peers * 8), BF),
                 VMEM((peers, 8, 128), BF),
                 VMEM((peers, 8, 128), BF),
                 VMEM((rows, peers * slots), BF),
@@ -753,10 +770,8 @@
                 DMA((4, 2 * planes)),
                 DMA((2 * planes,)),
                 DMA((2 * planes,)),
-                DMA,
-                DMA,
-                DMA((planes - 1,)),
-                DMA((planes - 1,)),
+                DMA((2 * planes,)),
+                DMA((2 * planes,)),
                 DMA,
                 DMA,
             ],

time: 145 us -> 142 us (0.979)
  Pallas kernels: 144 us -> 140 us
    pallas_call x1, Pallas kernels: 144 us -> 140 us  [on_device(): pl.pallas_call(functools.partial(layer, planes, peers), out_shape=jax.Sha...]
where the time goes in v7:
time: 142 us
  Pallas kernels  140 us (99%)
  local copies, waits for them, and re-layouts  1.57 us (1%)
    pallas_call x1, Pallas kernels, on_device(): pl.pallas_call(functools.partial(layer, planes, peers), out_shape=jax.Sha...  140 us

profile of v7, /device:TPU:1, one launch (start us, length us, event | category | flops | bytes accessed | tf_op | source)
XLA Modules:
  0.0 142.0 jit_solution(5798710011671657373)
XLA Ops:
  0.0 140.4 %shard_map.109 = bf16[128,512]{1,0:T(8,128)(2,1)} custom-call(bf16[128,512]{1,0:T(8,128)(2,1)} %attn_hbm.1, bf16[512,2048]{1,0:T(8,128)(2,1)} %proj_hbm.1, bf16[128,2048]{1,0:T(8,128)(2,1)} %hidden_hbm.1, bf16[2048]{0:T(1024)(128)(2,1)} %gain_hbm.1, bf16[64,2048]{1,0:T(8,128)(2,1)} %bitcast.3, s32[8,128]{1,0:T(8,128)} %bitcast.4, ...), custom_call_target="tpu_custom_call" | custom-call | tf_op jit(solution)/shard_map/pallas_call | solution.py:712
  140.4 1.6 %copy.13 = bf16[128,512]{1,0:T(8,128)(2,1)} copy(bf16[128,512]{1,0:T(8,128)(2,1)} %shard_map.109) | data formatting | bytes 262144

commit v8 on v7

--- a/solution.py
+++ b/solution.py
@@ -72,6 +72,7 @@
     taken_ref,
     pack_pick,
     out_pick,
+    out_block,
     pack_send,
     pack_recv,
     high,
@@ -149,17 +150,24 @@
         for i, (src, dst) in enumerate(
             [
                 (attn_hbm, attn_ref),
-                (proj_hbm, proj_ref),
+                (source_hbm, source_ref),
                 (hidden_hbm, hidden_ref),
                 (router_hbm, router_ref),
                 (routes_hbm, routes_ref),
                 (gain_hbm, gain_ref),
                 (last_gain_hbm, last_gain_ref),
-                (source_hbm, source_ref),
             ]
         )
     ]
-    for copy in inputs:
+    proj_cols = [
+        pl.ds(pl.multiple_of(lax.rem(x + d, planes) * share, share), share) for d in (2, 1, 3, 0)
+    ]
+    proj_in = [
+        pltpu.make_async_copy(proj_hbm.at[:, cols], proj_ref.at[:, cols], in_sem.at[7 + i])
+        for i, cols in enumerate(proj_cols)
+    ]
+    inputs[0].start()
+    for copy in proj_in + inputs[1:]:
         copy.start()
 
     piece = share // planes
@@ -196,17 +204,14 @@
             for copy in own_down(c, stage):
                 copy.start()
 
-    inputs[7].wait()
-    ask_send[...] = jnp.broadcast_to(source_ref[...], ask_send.shape)
     inputs[0].wait()
-    inputs[1].wait()
-    for j in range(planes):
-        part[j] = dot(attn_ref[...], proj_ref[:, j * share : (j + 1) * share])
+    proj_in[0].wait()
+    far_part = dot(attn_ref[...], proj_ref[:, proj_cols[0]])
     top, bottom = pl.ds(0, rows // 2), pl.ds(rows // 2, rows // 2)
     wing = share // 2
     wings = [pl.ds(0, wing), pl.ds(wing, wing)]
     for h in range(2):
-        far_send[h] = part[lax.rem(x + 2, planes), :, wings[h]].astype(BF)
+        far_send[h] = far_part[:, h * wing : (h + 1) * wing].astype(BF)
 
     pl.semaphore_wait(barrier, planes - 1 + 1 + peers - 1)
 
@@ -221,6 +226,11 @@
     ]
     for copy in far[0] + far[1]:
         copy.start()
+    for d, copy, cols in zip((1, 3, 0), proj_in[1:], proj_cols[1:]):
+        copy.wait()
+        part[lax.rem(x + d, planes)] = dot(attn_ref[...], proj_ref[:, cols])
+    inputs[1].wait()
+    ask_send[...] = jnp.broadcast_to(source_ref[...], ask_send.shape)
 
     middle = width // 4
     units_of = [(gates, gate_hbm, first) for first in range(0, width, middle)]
@@ -509,20 +519,33 @@
 
     activate(3, 0)
 
-    groups = [[0], [1]] + [[c, c + 1] for c in range(2, chunks - 2, 2)] + [[chunks - 2], [chunks - 1]]
-    group_of = {c: g for g, group in enumerate(groups) for c in group}
+    groups = [[0], [1]] + [[c, c + 1] for c in range(2, chunks - 2, 2)] + [[chunks - 2]]
+    groups += [[chunks - 1], [chunks - 1]]
+    final = len(groups) - 2
+    group_of = {c: g for g, group in enumerate(groups[:-1]) for c in group}
+    both = pl.ds(0, 2 * piece)
+
+    def columns(g):
+        return pl.ds((g - final) * piece, piece) if g >= final else both
 
     def back_copy(g, here, there, peer):
         first = groups[g][0]
+        pair, at = first // 2, first % 2
         if len(groups[g]) == 1:
-            src, dst = back_send.at[first // 2, here, first % 2], back_recv.at[first // 2, there, first % 2]
+            src = back_send.at[pair, here, at, :, columns(g)]
+            dst = back_recv.at[pair, there, at, :, columns(g)]
         else:
-            src, dst = back_send.at[first // 2, here], back_recv.at[first // 2, there]
+            src, dst = back_send.at[pair, here], back_recv.at[pair, there]
         return to_peer(src, dst, back_s.at[g], back_r.at[g], peer)
 
-    def mix_copy(c, d):
+    def mix_copy(c, d, cols=both, sem=None):
+        sem = c if sem is None else sem
         return to_plane(
-            mix_send.at[c], mix_recv.at[c, d - 1], mix_s.at[c], mix_r.at[c], lax.rem(x + d, planes)
+            mix_send.at[c, :, cols],
+            mix_recv.at[c, d - 1, :, cols],
+            mix_s.at[sem],
+            mix_r.at[sem],
+            lax.rem(x + d, planes),
         )
 
     def combine(c):
@@ -534,6 +557,17 @@
         total[c] = mixed
         for d in range(1, planes):
             mix_copy(c, d).start()
+
+    def combine_half(i):
+        c = chunks - 1
+        back_copy(final + i, everyone, everyone, me).wait_recv()
+        there = slice(i * piece, (i + 1) * piece)
+        back = back_recv[c // 2, :, c % 2, :, there].reshape(all_slots, piece)
+        mixed = dot(high[...], back) + dot(low[...], back)
+        mix_send[c, :, there] = mixed.astype(BF)
+        total[c, :, there] = mixed
+        for d in range(1, planes):
+            mix_copy(c, d, columns(final + i), c + i).start()
 
     three = pl.ds(0, planes - 1)
 
@@ -548,6 +582,18 @@
         added = whole[:, :piece] * whole[:, :piece] + whole[:, piece:] * whole[:, piece:]
         squares[...] = added if c == 0 else squares[...] + added
 
+    def finish_half(i):
+        c = chunks - 1
+        there = slice(i * piece, (i + 1) * piece)
+        cols = columns(final + i)
+        landing = mix_recv.at[c, three, :, cols]
+        to_plane(landing, landing, mix_s.at[c + i], mix_r.at[c + i], x).wait_recv()
+        whole = total[c, :, there] + res[c % 2 * 2 + i, :, c // 2 * piece : (c // 2 + 1) * piece].astype(F32)
+        for d in range(planes - 1):
+            whole = whole + mix_recv[c, d, :, there].astype(F32)
+        total[c, :, there] = whole
+        squares[...] = squares[...] + whole * whole
+
     def chunk_ready(c):
         @pl.when(host)
         def _():
@@ -581,11 +627,11 @@
     take_rows(1)
     for q in range(planes):
         activate(q, 1)
+    pass_down(1)
     produce(0, 1)
     send_back(0, 1)
-    pass_down(1)
     for c in range(1, chunks):
-        if c + 1 < chunks:
+        if 1 < c < chunks - 1:
             pass_down(c + 1)
         chunk_ready(c)
         g = group_of[c]
@@ -594,6 +640,11 @@
             produce(c, h)
             if last:
                 send_back(g, h)
+        if c == chunks - 1:
+            for h in range(2):
+                send_back(g + 1, h)
+        if c == 1:
+            pass_down(2)
         if c >= 4:
             combine(c - 4)
         if c >= 5:
@@ -622,10 +673,14 @@
     for c in range(planes):
         out_pick[c] = jnp.where(at == place + c, 1.0, 0.0).astype(BF)
 
-    for c in range(chunks - 4, chunks):
+    for c in range(chunks - 4, chunks - 1):
         combine(c)
         finish(c - 1)
-    finish(chunks - 1)
+    combine_half(0)
+    finish(chunks - 2)
+    combine_half(1)
+    finish_half(0)
+    finish_half(1)
     square = jnp.sum(squares[...], axis=1, keepdims=True)
     scale = lax.rsqrt(square / width + epsilon)
     packed = jnp.zeros((peers * 8, piece), F32)
@@ -675,13 +730,21 @@
     to_peer(slot_send.at[everyone], slot_recv.at[everyone], slot_s, slot_r, me).wait_send()
     for g in range(len(groups)):
         back_copy(g, everyone, everyone, me).wait_send()
-    for c in range(chunks):
-        for d in range(1, planes):
+    for d in range(1, planes):
+        for c in range(chunks - 1):
             mix_copy(c, d).wait_send()
+        for i in range(2):
+            mix_copy(chunks - 1, d, columns(final + i), chunks - 1 + i).wait_send()
     to_peer(pack_send.at[everyone], pack_recv.at[everyone], pack_s, pack_r, me).wait_recv()
     landed = pack_recv[...].reshape(peers * 8, 128)
+    outs = []
     for c in range(planes):
-        out_ref[:, c * piece : (c + 1) * piece] = dot(out_pick[c], landed).astype(BF)
+        cols = pl.ds(c * piece, piece)
+        out_block[:, c * piece : (c + 1) * piece] = dot(out_pick[c], landed).astype(BF)
+        outs.append(pltpu.make_async_copy(out_block.at[:, cols], out_ref.at[:, cols], in_sem.at[c]))
+        outs[c].start()
+    for copy in outs:
+        copy.wait()
 
     to_peer(pack_send.at[everyone], pack_recv.at[everyone], pack_s, pack_r, me).wait_send()
 
@@ -707,13 +770,12 @@
         top = routes.shape[1]
         slots = min(rows, 2 * rows * top // peers) // planes
         units = w_gate.shape[2]
-        local = pl.BlockSpec(memory_space=pltpu.VMEM)
         remote = pl.BlockSpec(memory_space=pl.ANY)
         return pl.pallas_call(
             functools.partial(layer, planes, peers),
             out_shape=jax.ShapeDtypeStruct((rows, share), BF),
             in_specs=[remote] * 11,
-            out_specs=local,
+            out_specs=remote,
             scratch_shapes=[
                 VMEM((rows, share), BF),
                 VMEM((share, width), BF),
@@ -750,11 +812,12 @@
                 VMEM((rows, peers * slots), BF),
                 VMEM((planes, peers * 8, rows), BF),
                 VMEM((planes, rows, peers * 8), BF),
+                VMEM((rows, share), BF),
                 VMEM((peers, 8, 128), BF),
                 VMEM((peers, 8, 128), BF),
                 VMEM((rows, peers * slots), BF),
                 VMEM((rows, peers * slots), BF),
-                DMA((8,)),
+                DMA((7 + planes,)),
                 DMA((3 + 4 * planes,)),
                 DMA((2, 4)),
                 DMA((2, 4)),
@@ -770,8 +833,8 @@
                 DMA((4, 2 * planes)),
                 DMA((2 * planes,)),
                 DMA((2 * planes,)),
-                DMA((2 * planes,)),
-                DMA((2 * planes,)),
+                DMA((2 * planes + 1,)),
+                DMA((2 * planes + 1,)),
                 DMA,
                 DMA,
             ],

time: 142 us -> 142 us (level)
  no operation moved by 1% of the time
where the time goes in v8:
time: 142 us
  Pallas kernels  140 us (99%)
  local copies, waits for them, and re-layouts  1.57 us (1%)
    pallas_call x1, Pallas kernels, on_device(): pl.pallas_call(functools.partial(layer, planes, peers), out_shape=jax.Sha...  140 us

profile of v8, /device:TPU:1, one launch (start us, length us, event | category | flops | bytes accessed | tf_op | source)
XLA Modules:
  0.0 141.7 jit_solution(17210351743406388486)
XLA Ops:
  0.0 140.1 %shard_map.109 = bf16[128,512]{1,0:T(8,128)(2,1)} custom-call(bf16[128,512]{1,0:T(8,128)(2,1)} %attn_hbm.1, bf16[512,2048]{1,0:T(8,128)(2,1)} %proj_hbm.1, bf16[128,2048]{1,0:T(8,128)(2,1)} %hidden_hbm.1, bf16[2048]{0:T(1024)(128)(2,1)} %gain_hbm.1, bf16[64,2048]{1,0:T(8,128)(2,1)} %bitcast.3, s32[8,128]{1,0:T(8,128)} %bitcast.4, ...), custom_call_target="tpu_custom_call" | custom-call | tf_op jit(solution)/shard_map/pallas_call | solution.py:774
  140.1 1.6 %copy.13 = bf16[128,512]{1,0:T(8,128)(2,1)} copy(bf16[128,512]{1,0:T(8,128)(2,1)} %shard_map.109) | data formatting | bytes 262144

commit v9 on v8

--- a/solution.py
+++ b/solution.py
@@ -246,7 +246,7 @@
         return to_device(
             hbm.at[0, pl.ds(base + first, count)],
             buffer.at[slot, pl.ds(base + first, count)],
-            w_s.at[kind, u],
+            w_s,
             w_r.at[slot, u],
             plane,
             peer,
@@ -254,7 +254,7 @@
 
     def onward_unit(u, slot, there, kind, plane, peer):
         return to_device(
-            unit_view(slot, u), unit_view(there, u), w_s.at[kind, u], w_r.at[there, u], plane, peer
+            unit_view(slot, u), unit_view(there, u), w_s, w_r.at[there, u], plane, peer
         )
 
     def unit_arrived(slot, u):
@@ -413,7 +413,7 @@
 
     def chunk_copy(c, source, slot, kind, plane, peer):
         return to_device(
-            source.at[c], downs.at[slot, c], d_s.at[kind, c], d_r.at[slot, c], plane, peer
+            source.at[c], downs.at[slot, c], d_s, d_r.at[slot, c], plane, peer
         )
 
     def chunk_arrived(slot, c):
@@ -543,7 +543,7 @@
         return to_plane(
             mix_send.at[c, :, cols],
             mix_recv.at[c, d - 1, :, cols],
-            mix_s.at[sem],
+            mix_s,
             mix_r.at[sem],
             lax.rem(x + d, planes),
         )
@@ -572,7 +572,7 @@
     three = pl.ds(0, planes - 1)
 
     def finish(c):
-        to_plane(mix_recv.at[c, three], mix_recv.at[c, three], mix_s.at[c], mix_r.at[c], x).wait_recv()
+        to_plane(mix_recv.at[c, three], mix_recv.at[c, three], mix_s, mix_r.at[c], x).wait_recv()
         at = slice(c // 2 * piece, (c // 2 + 1) * piece)
         first = c % 2 * 2
         whole = total[c] + jnp.concatenate([res[first, :, at], res[first + 1, :, at]], axis=1).astype(F32)
@@ -587,7 +587,7 @@
         there = slice(i * piece, (i + 1) * piece)
         cols = columns(final + i)
         landing = mix_recv.at[c, three, :, cols]
-        to_plane(landing, landing, mix_s.at[c + i], mix_r.at[c + i], x).wait_recv()
+        to_plane(landing, landing, mix_s, mix_r.at[c + i], x).wait_recv()
         whole = total[c, :, there] + res[c % 2 * 2 + i, :, c // 2 * piece : (c // 2 + 1) * piece].astype(F32)
         for d in range(planes - 1):
             whole = whole + mix_recv[c, d, :, there].astype(F32)
@@ -827,13 +827,13 @@
                 DMA,
                 DMA,
                 DMA((2,)),
+                DMA,
                 DMA((4, 8)),
-                DMA((4, 8)),
-                DMA((4, 2 * planes)),
+                DMA,
                 DMA((4, 2 * planes)),
                 DMA((2 * planes,)),
                 DMA((2 * planes,)),
-                DMA((2 * planes + 1,)),
+                DMA,
                 DMA((2 * planes + 1,)),
                 DMA,
                 DMA,

time: 142 us -> 141 us (level)
  no operation moved by 1% of the time
where the time goes in v9:
time: 141 us
  Pallas kernels  139 us (99%)
  local copies, waits for them, and re-layouts  1.57 us (1%)
    pallas_call x1, Pallas kernels, on_device(): pl.pallas_call(functools.partial(layer, planes, peers), out_shape=jax.Sha...  139 us

profile of v9, /device:TPU:1, one launch (start us, length us, event | category | flops | bytes accessed | tf_op | source)
XLA Modules:
  0.0 141.0 jit_solution(2668055245356257300)
XLA Ops:
  0.0 139.5 %shard_map.109 = bf16[128,512]{1,0:T(8,128)(2,1)} custom-call(bf16[128,512]{1,0:T(8,128)(2,1)} %attn_hbm.1, bf16[512,2048]{1,0:T(8,128)(2,1)} %proj_hbm.1, bf16[128,2048]{1,0:T(8,128)(2,1)} %hidden_hbm.1, bf16[2048]{0:T(1024)(128)(2,1)} %gain_hbm.1, bf16[64,2048]{1,0:T(8,128)(2,1)} %bitcast.3, s32[8,128]{1,0:T(8,128)} %bitcast.4, ...), custom_call_target="tpu_custom_call" | custom-call | tf_op jit(solution)/shard_map/pallas_call | solution.py:774
  139.5 1.6 %copy.13 = bf16[128,512]{1,0:T(8,128)(2,1)} copy(bf16[128,512]{1,0:T(8,128)(2,1)} %shard_map.109) | data formatting | bytes 262144

commit v10 on v9

--- a/solution.py
+++ b/solution.py
@@ -271,12 +271,12 @@
 
         @pl.when(host)
         def _():
-            for u, first, count in spans((128, 256, 384)):
+            for u, first, count in spans((256, 512, 768)):
                 own_unit(u, 1, 0, partner, me, first, count).start()
 
         @pl.when(guest)
         def _():
-            for u, first, count in spans((128, 256, 384)):
+            for u, first, count in spans((256, 512, 768)):
                 own_unit(u, 2, 0, outer, sibling, first, count).start()
 
     send_rows(0)

time: 141 us -> 141 us (level)
  no operation moved by 1% of the time
where the time goes in v10:
time: 141 us
  Pallas kernels  139 us (99%)
  local copies, waits for them, and re-layouts  1.57 us (1%)
    pallas_call x1, Pallas kernels, on_device(): pl.pallas_call(functools.partial(layer, planes, peers), out_shape=jax.Sha...  139 us

profile of v10, /device:TPU:1, one launch (start us, length us, event | category | flops | bytes accessed | tf_op | source)
XLA Modules:
  0.0 140.8 jit_solution(3694438031238286466)
XLA Ops:
  0.0 139.2 %shard_map.109 = bf16[128,512]{1,0:T(8,128)(2,1)} custom-call(bf16[128,512]{1,0:T(8,128)(2,1)} %attn_hbm.1, bf16[512,2048]{1,0:T(8,128)(2,1)} %proj_hbm.1, bf16[128,2048]{1,0:T(8,128)(2,1)} %hidden_hbm.1, bf16[2048]{0:T(1024)(128)(2,1)} %gain_hbm.1, bf16[64,2048]{1,0:T(8,128)(2,1)} %bitcast.3, s32[8,128]{1,0:T(8,128)} %bitcast.4, ...), custom_call_target="tpu_custom_call" | custom-call | tf_op jit(solution)/shard_map/pallas_call | solution.py:774
  139.2 1.6 %copy.13 = bf16[128,512]{1,0:T(8,128)(2,1)} copy(bf16[128,512]{1,0:T(8,128)(2,1)} %shard_map.109) | data formatting | bytes 262144
